TPU v7x, 128 devices: a whole 4x4x4 slice. The times are simulated.
128 devices in a mesh: seq: 16 (over z, y), head: 8 (over x, core).
Axes of the slice: x: 4, y: 4, z: 4, core: 2. Of those that a mesh axis runs over, the one named last changes fastest.
Arguments:
- hidden: bfloat16 [8192, 8192], P('seq'), may hold values from -6 to 6
- w_query: bfloat16 [8192, 4096], P('seq', 'head'), may hold values from -0.0625 to 0.0625
- w_key: bfloat16 [8192, 4096], P('seq', 'head'), may hold values from -0.0625 to 0.0625
- w_value: bfloat16 [8192, 4096], P('seq', 'head'), may hold values from -0.0625 to 0.0625
- cotangent: bfloat16 [8192, 4096], P('seq', 'head'), may hold values from -6 to 6
Outputs:
- step_direction: float32 [8192, 8192], P(('seq', 'head'))
All inputs are finite; a program needn't handle non-finite values.
Results may differ from a plain program's by a relative error of at most 0.015.
Values may be sent and summed in bfloat16 or wider, within the bound.
No kernel may reach another device: no remote copies, remote signals or barrier semaphores. Data moves between devices by JAX's collectives and lax.ppermute only.
A program may use at most 192 MiB of HBM per device.

v0:
```python
import functools

import jax
import jax.numpy as jnp
from jax import lax
from jax.experimental import pallas as pl
from jax.experimental.pallas import tpu as pltpu
from jax.sharding import Mesh
from jax.sharding import PartitionSpec as P

DH = 128
SEQ = ("z", "y")
HEAD = ("x", "c")
NORM_EPS = 1e-05
STEP_EPS = 1e-06
BF = jnp.bfloat16
F32 = jnp.float32
ORDERS = (
    ((("z", 1), ("z", 3), ("y", 1), ("y", 3)), (("z", 3), ("z", 1), ("y", 3), ("y", 1))),
    ((("y", 1), ("y", 3), ("z", 1), ("z", 3)), (("y", 3), ("y", 1), ("z", 3), ("z", 1))),
)
PARTS = ((0, 8), (8, 12), (12, 16))
NT = (((1,), (1,)), ((), ()))
TN = (((0,), (0,)), ((), ()))


def swap(x, axis, offset):
    n = lax.axis_size(axis)
    return lax.ppermute(x, axis, [(i, i ^ offset) for i in range(n)])


def swap_links(x, half, step):
    pairs = []
    for z in range(4):
        for y in range(4):
            for c in range(2):
                axis, o = ORDERS[half][c][step]
                to_z, to_y = (z ^ o, y) if axis == "z" else (z, y ^ o)
                pairs.append(((z * 4 + y) * 2 + c, (to_z * 4 + to_y) * 2 + c))
    return lax.ppermute(x, ("z", "y", "c"), pairs)


def slot_offsets(half, core):
    inner, outer = ORDERS[half][0][0][0], ORDERS[half][0][2][0]
    slots = []
    for group in (0, 1, 3, 2) if core == 0 else (0, 3, 1, 2):
        for o in (0, 1, 3, 2):
            offset = {inner: o, outer: group}
            slots.append((offset["z"], offset["y"]))
    return slots


def sources(half, core):
    z, y = lax.axis_index("z"), lax.axis_index("y")
    return jnp.stack([((z ^ dz) * 4 + (y ^ dy)) * 2 + half for dz, dy in slot_offsets(half, core)])


def own_sources():
    c = lax.axis_index("c")
    return jnp.stack([jnp.where(c == 0, sources(h, 0), sources(h, 1)) for h in (0, 1)]).astype(jnp.int32)


def after(x, *others):
    return lax.optimization_barrier((x, *others))[0]


def join(held, got, step):
    if step != 1:
        return jnp.concatenate([held, got], axis=0)
    n = 1
    first = lax.axis_index("c") == 0
    inner = [jnp.where(first, held[n:], got[:n]), jnp.where(first, got[:n], held[n:])]
    return jnp.concatenate([held[:n], *inner, got[n:]], axis=0)


def gather(block, ready):
    held = [block[:1], block[1:]]
    for step in (0, 1):
        got = [swap_links(held[h], h, step) for h in (0, 1)]
        held = [join(held[h], got[h], step) for h in (0, 1)]
    near = [swap_links(held[h], h, 2) for h in (0, 1)]
    far = [swap_links(after(held[h], *ready), h, 3) for h in (0, 1)]
    wide = 2 * block.shape[1] // 3
    last_kv = [swap_links(near[h][:, :wide], h, 3) for h in (0, 1)]
    last_q = [swap_links(near[h][:, wide:], h, 3) for h in (0, 1)]
    return held, near, far, last_kv, last_q


def reorder_kernel(table, a, b, *outs):
    k = pl.program_id(0)
    for h, src in enumerate((a, b)):
        turned = src[...].T
        for p, (lo, hi) in enumerate(PARTS):

            @pl.when((k >= lo) & (k < hi))
            def _(out=outs[3 * h + p], turned=turned):
                out[0] = turned


def reorder_columns(hidden, table):
    rows, width = hidden.shape
    q = width // 32
    take = lambda h: pl.BlockSpec((rows, q), lambda k, t, h=h: (0, t[h, k]))
    give = [
        pl.BlockSpec((1, q, rows), lambda k, t, lo=lo, n=hi - lo: (jnp.clip(k - lo, 0, n - 1), 0, 0)) for lo, hi in PARTS
    ]
    return pl.pallas_call(
        reorder_kernel,
        grid_spec=pltpu.PrefetchScalarGridSpec(
            num_scalar_prefetch=1, grid=(16,), in_specs=[take(0), take(1)], out_specs=give * 2
        ),
        out_shape=[jax.ShapeDtypeStruct((hi - lo, q, rows), hidden.dtype) for lo, hi in PARTS] * 2,
        cost_estimate=pl.CostEstimate(flops=0, bytes_accessed=4 * rows * width, transcendentals=0),
        compiler_params=pltpu.CompilerParams(vmem_limit_bytes=2 << 20),
        name="reorder_columns",
    )(table, hidden, hidden)


def finish_kernel(table, a, b, c, d, out):
    parts = (a, b, c, d)
    total = sum(jnp.sum(jnp.square(p[...].astype(F32)), axis=-1, keepdims=True) for p in parts)
    factor = lax.rsqrt(total / out.shape[1] + STEP_EPS)
    for v, p in enumerate(parts):
        for k in range(8):
            cols = pl.ds(pl.multiple_of(table[v * 8 + k] * 256, 256), 256)
            out[:, cols] = jnp.tanh(p[:, k * 256 : (k + 1) * 256].astype(F32) * factor)


def finish(parts, table):
    rows = parts[0].shape[0]
    width = 4 * parts[0].shape[1]
    return pl.pallas_call(
        finish_kernel,
        in_specs=[pl.BlockSpec(memory_space=pltpu.SMEM)] + [pl.BlockSpec(memory_space=pltpu.VMEM)] * 4,
        out_specs=pl.BlockSpec(memory_space=pltpu.VMEM),
        out_shape=jax.ShapeDtypeStruct((rows, width), F32),
        compiler_params=pltpu.CompilerParams(vmem_limit_bytes=10 << 20),
        name="finish",
    )(table, *parts)


def state_round(own, axis, reverse):
    here = lax.axis_index(axis)
    sent = own.astype(BF)
    inside = jnp.zeros_like(own)
    total = own
    for o in (1, 3, 2):
        other = swap(sent, axis, o).astype(F32)
        there = here ^ o
        inside = inside + jnp.where(there > here if reverse else there < here, other, 0.0)
        total = total + other
    return inside, total


def sigmoid(a):
    return 1.0 / (1.0 + jnp.exp(-a))


def silu_slope(preact):
    gate = sigmoid(preact)
    return gate * (1.0 + preact * (1.0 - gate))


def dot(a, b, dims=(((1,), (0,)), ((), ()))):
    return lax.dot_general(a, b, dims, preferred_element_type=F32)


def causal_mask(n):
    return lax.broadcasted_iota(jnp.int32, (n, n), 0) <= lax.broadcasted_iota(jnp.int32, (n, n), 1)


def side_by_side(w):
    return jnp.concatenate([w[k] for k in range(w.shape[0])], axis=1)


def project_kernel(slots, starts, heads, *refs):
    count = len(slots)
    begins, refs = refs[:starts], refs[starts:]
    weights, hids, outs = refs[:count], refs[count : count + 2], refs[count + 2 : -3]
    buf, hid_buf, sems = refs[-3:]
    copies = []
    for i, (half, slot) in enumerate(slots):
        copies.append(pltpu.make_async_copy(weights[i], buf.at[i], sems.at[i]))
        copies.append(pltpu.make_async_copy(hids[half].at[pl.ds(slot, 4)], hid_buf.at[i], sems.at[count + i]))
    for copy in copies:
        copy.start()
    sums = outs[:-1] if heads else outs
    for i in range(count):
        copies[2 * i].wait()
        copies[2 * i + 1].wait()
        t = dot(side_by_side(buf[i]), hid_buf[i].reshape(-1, hid_buf.shape[3]))
        at = 0
        for j, out in enumerate(sums):
            part = t[at : at + out.shape[0]]
            at += out.shape[0]
            if i:
                out[...] += part
            else:
                out[...] = begins[j][...] + part if starts else part

    for h in range(heads):
        out = outs[0]
        pk = out[h * DH : (h + 1) * DH, :]
        k = (pk * sigmoid(pk)).astype(BF)
        v = out[(heads + h) * DH : (heads + h + 1) * DH, :].astype(BF)
        outs[-1][h] = dot(k, v, NT)


def project(limit, weights, slots, hid, widths, start=(), heads=0):
    cols, q = weights[0].shape[1:]
    n = hid[0].shape[2]
    vmem = pl.BlockSpec(memory_space=pltpu.VMEM)
    anywhere = pl.BlockSpec(memory_space=pltpu.HBM)
    out_shape = [jax.ShapeDtypeStruct((w, n), F32) for w in widths]
    if heads:
        out_shape.append(jax.ShapeDtypeStruct((heads, DH, DH), F32))
    count = len(slots)
    return pl.pallas_call(
        functools.partial(project_kernel, slots, len(start), heads),
        in_specs=[vmem] * len(start) + [anywhere] * (count + 2),
        out_specs=[vmem] * len(out_shape),
        out_shape=out_shape,
        scratch_shapes=[
            pltpu.VMEM((count, 4, cols, q), BF),
            pltpu.VMEM((count, 4, q, n), BF),
            pltpu.SemaphoreType.DMA((2 * count,)),
        ],
        cost_estimate=pl.CostEstimate(
            flops=8 * count * cols * q * n, bytes_accessed=8 * count * cols * q, transcendentals=0
        ),
        compiler_params=pltpu.CompilerParams(vmem_limit_bytes=limit << 20),
        name="project",
    )(*start, *weights, *hid)


def attend_kernel(pre_q, pre_k, pre_v, before, cot, own_grad, grad_att):
    pq = pre_q[...]
    pk = pre_k[...]
    q = (pq * sigmoid(pq)).astype(BF)
    k = (pk * sigmoid(pk)).astype(BF)
    v = pre_v[...].astype(BF)
    b = before[0].astype(BF)
    scores = jnp.where(causal_mask(q.shape[1]), dot(k, q, TN), 0.0).astype(BF)
    attended = dot(v, scores) + dot(b, q, TN)
    scale = lax.rsqrt(jnp.mean(attended * attended, axis=0, keepdims=True) + NORM_EPS)
    normed = attended * scale
    up = cot[...].T.astype(F32)
    ga = (scale * (up - normed * jnp.mean(up * normed, axis=0, keepdims=True))).astype(BF)
    grad_att[...] = ga
    own_grad[0] = dot(q, ga, NT)


def attend_back_kernel(pre_q, pre_k, pre_v, before, grad_att, back_q, grad_k, grad_v):
    pq = pre_q[...]
    pk = pre_k[...]
    q = (pq * sigmoid(pq)).astype(BF)
    k = (pk * sigmoid(pk)).astype(BF)
    v = pre_v[...].astype(BF)
    b = before[0].astype(BF)
    ga = grad_att[...]
    causal = causal_mask(q.shape[1])
    scores = jnp.where(causal, dot(k, q, TN), 0.0).astype(BF)
    gs = jnp.where(causal, dot(v, ga, TN), 0.0).astype(BF)
    gq = dot(k, gs) + dot(b, ga)
    back_q[...] = (gq * silu_slope(pq)).astype(BF)
    grad_k[...] = dot(q, gs, NT)
    grad_v[...] = dot(ga, scores, NT)


def head_specs(n, heads):
    row = pl.BlockSpec((DH, n), lambda h: (h, 0))
    row_v = pl.BlockSpec((DH, n), lambda h: (heads + h, 0))
    state = pl.BlockSpec((1, DH, DH), lambda h: (h, 0, 0))
    return row, row_v, state


def attend(pre_query, pre_kv, before, cotangent):
    width, n = pre_query.shape
    heads = width // DH
    row, row_v, state = head_specs(n, heads)
    return pl.pallas_call(
        attend_kernel,
        grid=(heads,),
        in_specs=[row, row, row_v, state, pl.BlockSpec((n, DH), lambda h: (0, h))],
        out_specs=[state, row],
        out_shape=[
            jax.ShapeDtypeStruct((heads, DH, DH), F32),
            jax.ShapeDtypeStruct((width, n), BF),
        ],
        compiler_params=pltpu.CompilerParams(vmem_limit_bytes=4 << 20),
        name="attend",
    )(pre_query, pre_kv, pre_kv, before, cotangent)


def attend_back(pre_query, pre_kv, before, grad_att):
    width, n = pre_query.shape
    heads = width // DH
    row, row_v, state = head_specs(n, heads)
    return pl.pallas_call(
        attend_back_kernel,
        grid=(heads,),
        in_specs=[row, row, row_v, state, row],
        out_specs=[row, row, row],
        out_shape=[
            jax.ShapeDtypeStruct((width, n), BF),
            jax.ShapeDtypeStruct((width, n), F32),
            jax.ShapeDtypeStruct((width, n), F32),
        ],
        cost_estimate=pl.CostEstimate(flops=6 * heads * n * n * DH, bytes_accessed=16 * n * width, transcendentals=0),
        compiler_params=pltpu.CompilerParams(vmem_limit_bytes=4 << 20),
        name="attend_back",
    )(pre_query, pre_kv, pre_kv, before, grad_att)


def row_order(first):
    second = 4 - first
    return [(ox, oc) for oc in (1, 0) for ox in (0, second, first, 2)]


def collect_kernel(table, pre_kv, grad_k, grad_v, back_q, later, rows1, rows3, back):
    width, n = back_q.shape
    for h in range(width // DH):
        cols = slice(h * DH, (h + 1) * DH)
        vcols = slice(width + h * DH, width + (h + 1) * DH)
        qcols = slice(2 * width + h * DH, 2 * width + (h + 1) * DH)
        pk = pre_kv[cols, :]
        k = (pk * sigmoid(pk)).astype(BF)
        v = pre_kv[vcols, :].astype(BF)
        a = later[h].astype(BF)
        back[:, cols] = ((grad_k[cols, :] + dot(a, v)) * silu_slope(pk)).astype(BF).T
        back[:, vcols] = (grad_v[cols, :] + dot(a, k, TN)).astype(BF).T
        back[:, qcols] = back_q[cols, :].T
    g = n // 8
    for f, rows in enumerate((rows1, rows3)):
        for k in range(8):
            rows[k * g : (k + 1) * g, :] = back[pl.ds(pl.multiple_of(table[f * 8 + k] * g, g), g), :]


def collect(pre_kv, grad_k, grad_v, back_q, later):
    width, n = back_q.shape
    x, c = lax.axis_index("x"), lax.axis_index("c")
    table = jnp.stack([(x ^ ox) * 2 + (c ^ oc) for first in (1, 3) for ox, oc in row_order(first)]).astype(jnp.int32)
    return pl.pallas_call(
        collect_kernel,
        in_specs=[pl.BlockSpec(memory_space=pltpu.SMEM)] + [pl.BlockSpec(memory_space=pltpu.VMEM)] * 5,
        out_specs=[pl.BlockSpec(memory_space=pltpu.VMEM)] * 2,
        out_shape=[jax.ShapeDtypeStruct((n, 3 * width), BF)] * 2,
        scratch_shapes=[pltpu.VMEM((n, 3 * width), BF)],
        compiler_params=pltpu.CompilerParams(vmem_limit_bytes=8 << 20),
        name="collect",
    )(table, pre_kv, grad_k, grad_v, back_q, later)


def push_kernel(kind, rows_in, *refs):
    count = 2 if kind else 3
    other, mine = refs[count : count + 2]
    rows = refs[count + 2]
    bufs = refs[count + 3 : 2 * count + 3]
    other_buf, mine_buf, sems, out_sems, rows_sem = refs[2 * count + 3 :]
    half = other.shape[0]
    c = lax.axis_index("c")
    places = (c, 1 - c) if kind else (0, 1)
    take_rows = pltpu.make_async_copy(rows_in, rows, rows_sem)
    take_rows.start()
    sides = [[(refs[0], bufs[0], 0)], [(refs[1], bufs[1], 0)]]
    if not kind:
        sides[1].append((refs[2], bufs[2], refs[1].shape[1]))
    copies = []
    for i in range(4):
        at = pl.ds(2 * (i % 2), 2)
        copies.append(
            [
                pltpu.make_async_copy(src.at[at], buf.at[at], sems.at[2 * i + j])
                for j, (src, buf, _) in enumerate(sides[i // 2])
            ]
        )
    for group in copies:
        for copy in group:
            copy.start()
    take_rows.wait()
    outs = []
    for i in range(4):
        for copy in copies[i]:
            copy.wait()
        total = None
        for _, buf, at in sides[i // 2]:
            side = jnp.concatenate([buf[2 * (i % 2)], buf[2 * (i % 2) + 1]], axis=1)
            term = dot(rows[:, at : at + side.shape[0]], side)
            total = term if total is None else total + term
        other_buf[i] = total[:half].astype(other.dtype)
        mine_buf[i] = total[half:].astype(mine.dtype)
        cols = pl.ds(pl.multiple_of(places[i // 2] * 1024 + (i % 2) * 512, 512), 512)
        for j, (buf, out) in enumerate(((other_buf, other), (mine_buf, mine))):
            outs.append(pltpu.make_async_copy(buf.at[i], out.at[:, cols], out_sems.at[2 * i + j]))
            outs[-1].start()
    for copy in outs:
        copy.wait()


def push(kind, rows, weights):
    n = rows.shape[0]
    hbm = pl.BlockSpec(memory_space=pltpu.HBM)
    return pl.pallas_call(
        functools.partial(push_kernel, kind),
        in_specs=[hbm] * (1 + len(weights)),
        out_specs=[hbm] * 2,
        out_shape=[jax.ShapeDtypeStruct((n // 2, 2048), BF)] * 2,
        scratch_shapes=[
            pltpu.VMEM(rows.shape, BF),
            *(pltpu.VMEM(w.shape, BF) for w in weights),
            pltpu.VMEM((4, n // 2, 512), BF),
            pltpu.VMEM((4, n // 2, 512), BF),
            pltpu.SemaphoreType.DMA((8,)),
            pltpu.SemaphoreType.DMA((8,)),
            pltpu.SemaphoreType.DMA,
        ],
        cost_estimate=pl.CostEstimate(flops=2 * n * 1536 * 2048, bytes_accessed=1536 * 4096, transcendentals=0),
        compiler_params=pltpu.CompilerParams(vmem_limit_bytes=54 << 20),
        name="push",
    )(rows, *weights)


def transposed(w):
    return jnp.swapaxes(w.reshape(2, w.shape[0] // 2, w.shape[1]), 1, 2)


def on_device(hidden, w_query, w_key, w_value, cotangent):
    heads = w_query.shape[1] // DH
    n = hidden.shape[0]
    hid = reorder_columns(hidden, own_sources())
    block = jnp.concatenate([transposed(w_key), transposed(w_value), transposed(w_query)], axis=1)
    held, near, far, last_kv, last_q = gather(block, hid)
    wide = 2 * heads * DH
    sums = project(20, [held[0], near[0], held[1], near[1]], ((0, 0), (0, 4), (1, 0), (1, 4)), hid[0::3], (wide, wide // 2))
    sums = project(14, far, ((0, 0), (1, 0)), hid[1::3], (wide, wide // 2), sums)
    pre_kv, own_state = project(44, last_kv, ((0, 0), (1, 0)), hid[2::3], (wide,), sums[:1], heads)
    inner, total = state_round(own_state, "y", False)
    outer, _ = state_round(total, "z", False)
    before = inner + outer
    pre_query = project(44, last_q, ((0, 0), (1, 0)), hid[2::3], (wide // 2,), sums[1:])[0]
    own_grad, grad_att = attend(pre_query, pre_kv, before, cotangent)
    back_q, grad_k, grad_v = attend_back(pre_query, pre_kv, before, grad_att)
    inner, total = state_round(own_grad, "y", True)
    outer, _ = state_round(after(total, back_q), "z", True)
    later = inner + outer
    rows = collect(pre_kv, grad_k, grad_v, back_q, later)

    size = n // 8
    tables = []
    started = []
    for h in (0, 1):
        for kind in (0, 1):
            use = rows[kind]
            if len(started) >= 2:
                use = after(use, started[-2][0])
            other, mine = push(kind, use, (near[h], far[h]) if kind else (held[h], last_kv[h], last_q[h]))
            got = swap(other, "c", 1)
            send = (mine[2 * size :].astype(F32) + got[2 * size :].astype(F32)).astype(BF)
            started.append((send, mine, got, swap(send, "x", (1, 3)[kind])))
            src = sources(h, 0)
            picks = (0, 1, 2, 3, 12, 13, 14, 15) if kind == 0 else (4, 5, 6, 7, 8, 9, 10, 11)
            tables.append(jnp.stack([src[p] for p in picks]))
    middle = []
    for i, (send, mine, got, got2) in enumerate(started):
        keep = mine[: 2 * size].astype(F32) + got[: 2 * size].astype(F32) + got2.astype(F32)
        middle.append((keep, swap(keep[size:].astype(BF), "x", (3, 1)[i % 2])))
    parts = []
    for i, (keep, got3) in enumerate(middle):
        if i < 2:
            got3 = after(got3, started[2][0], started[3][0])
        parts.append(keep[:size] + got3.astype(F32))
    return finish(parts, jnp.concatenate(tables).astype(jnp.int32))


def solution(mesh):
    finer = Mesh(mesh.devices.reshape(4, 4, 4, 2), ("z", "y", "x", "c"))
    in_specs = (P(SEQ, None), P(SEQ, HEAD), P(SEQ, HEAD), P(SEQ, HEAD), P(SEQ, HEAD))
    out_specs = P(SEQ + HEAD, None)
    return jax.shard_map(on_device, mesh=finer, in_specs=in_specs, out_specs=out_specs, check_vma=False)
```

profile of v0, /device:TPU:0, one launch (start us, length us, event | category | flops | bytes accessed | tf_op | source)
XLA Modules:
  0.0 274.8 jit_solution(15117132807769403796)
XLA Ops:
  6.7 8.4 %collective-permute-done.3 = bf16[1,1536,256]{2,1,0:T(8,128)(2,1)S(1)} collective-permute-done((bf16[1,1536,256]{2,1,0:T(8,128)(2,1)S(1)}, bf16[1,1536,256]{2,1,0:T(8,128)(2,1)S(1)}, u32[]{:S(2)}, u32[]{:S(2)}) %collective-permute-start.3) | collective-permute-done | bytes 786464 | tf_op jit(solution)/shard_map/ppermute | solution.py:40
  16.3 3.1 %collective-permute-start.4 = (bf16[2,1536,256]{2,1,0:T(8,128)(2,1)}, bf16[2,1536,256]{2,1,0:T(8,128)(2,1)}, u32[]{:S(2)}, u32[]{:S(2)}) collective-permute-start(bf16[2,1536,256]{2,1,0:T(8,128)(2,1)} %pad_maximum_fusion.4), channel_id=1, source_target_pairs={{0,24},{1,9},{8,16},{9,1},{16,8},{17,25},{24,0},{25,17},{32,56},{3... | collective-permute-start | bytes 4718600 | tf_op jit(solution)/shard_map/ppermute | solution.py:40
  20.8 4.0 %collective-permute-start.1 = (bf16[2,1536,256]{2,1,0:T(8,128)(2,1)}, bf16[2,1536,256]{2,1,0:T(8,128)(2,1)}, u32[]{:S(2)}, u32[]{:S(2)}) collective-permute-start(bf16[2,1536,256]{2,1,0:T(8,128)(2,1)} %pad_maximum_fusion.3), channel_id=1, source_target_pairs={{0,96},{1,33},{8,104},{9,41},{16,112},{17,49},{24,120},{25,57},{32... | collective-permute-start | bytes 4718600 | tf_op jit(solution)/shard_map/ppermute | solution.py:40
  24.8 13.5 %collective-permute-done.4 = bf16[2,1536,256]{2,1,0:T(8,128)(2,1)} collective-permute-done((bf16[2,1536,256]{2,1,0:T(8,128)(2,1)}, bf16[2,1536,256]{2,1,0:T(8,128)(2,1)}, u32[]{:S(2)}, u32[]{:S(2)}) %collective-permute-start.4) | collective-permute-done | bytes 1572896 | tf_op jit(solution)/shard_map/ppermute | solution.py:40
  38.3 5.2 %collective-permute-done.1 = bf16[2,1536,256]{2,1,0:T(8,128)(2,1)} collective-permute-done((bf16[2,1536,256]{2,1,0:T(8,128)(2,1)}, bf16[2,1536,256]{2,1,0:T(8,128)(2,1)}, u32[]{:S(2)}, u32[]{:S(2)}) %collective-permute-start.1) | collective-permute-done | bytes 1572896 | tf_op jit(solution)/shard_map/ppermute | solution.py:40
  50.0 3.4 %copy-done = bf16[512,8192]{1,0:T(8,128)(2,1)S(1)} copy-done((bf16[512,8192]{1,0:T(8,128)(2,1)S(1)}, bf16[512,8192]{1,0:T(8,128)(2,1)}, u32[]{:S(2)}) %copy-start) | copy-done | bytes 8388632
  53.4 6.5 %reorder_columns.1 = (bf16[8,256,512]{2,1,0:T(8,128)(2,1)S(1)}, bf16[4,256,512]{2,1,0:T(8,128)(2,1)S(1)}, bf16[4,256,512]{2,1,0:T(8,128)(2,1)S(1)}, bf16[8,256,5...) custom-call(s32[2,16]{1,0:T(2,128)S(1)} %pad_add_fusion.table, ...), custom_call_target="tpu_custom_call" | custom-call | bytes 16777216 | tf_op jit(solution)/shard_map/reorder_columns/pallas_call | solution.py:107
  61.0 3.2 %collective-permute-start.7 = (bf16[4,1536,256]{2,1,0:T(8,128)(2,1)}, bf16[4,1536,256]{2,1,0:T(8,128)(2,1)S(1)}, u32[]{:S(2)}, u32[]{:S(2)}) collective-permute-start(bf16[4,1536,256]{2,1,0:T(8,128)(2,1)} %pad_maximum_fusion.1.refs_2_.refs_0_), channel_id=1, source_target_pairs={{0,96},{1,33},{8,104},{9,41},{16,112},{17,49},{24,120},{25,57},{32... | collective-permute-start | bytes 9437192 | tf_op jit(solution)/shard_map/ppermute | solution.py:40
  64.3 42.7 %collective-permute-done.2.refs_1_.refs_0_ = bf16[4,1536,256]{2,1,0:T(8,128)(2,1)} collective-permute-done((bf16[4,1536,256]{2,1,0:T(8,128)(2,1)}, bf16[4,1536,256]{2,1,0:T(8,128)(2,1)}, u32[]{:S(2)}, u32[]{:S(2)}) %collective-permute-start.2) | collective-permute-done | bytes 3145760 | tf_op jit(solution)/shard_map/ppermute | solution.py:40
  111.8 6.3 %collective-permute-start.9 = (bf16[4,1024,256]{2,1,0:T(8,128)(2,1)S(1)}, bf16[4,1024,256]{2,1,0:T(8,128)(2,1)S(1)}, u32[]{:S(2)}, u32[]{:S(2)}) collective-permute-start(bf16[4,1024,256]{2,1,0:T(8,128)(2,1)S(1)} %slice.149), channel_id=1, source_target_pairs={{0,96},{1,33},{8,104},{9,41},{16,112},{17,49},{24,120},{25,57},{32... | collective-permute-start | bytes 6291464 | tf_op jit(solution)/shard_map/ppermute | solution.py:40
  122.3 2.3 slice.151
  124.8 10.1 %project.4 = (f32[1024,512]{1,0:T(8,128)S(1)}, f32[512,512]{1,0:T(8,128)S(1)}) custom-call(bf16[4,1536,256]{2,1,0:T(8,128)(2,1)} %pad_maximum_fusion.refs_0_, bf16[4,1536,256]{2,1,0:T(8,128)(2,1)} %collective-permute-done.2.refs_1_.refs_0_, bf16[4,1536,256]{2,1,0:T(8,128)(2,1)} %pad_maximum_fusion.1.refs_2_.refs_0_, ...), custom_call_target="tpu_custom_call" | custom-call | flops 6442450944 | bytes 12582912 | tf_op jit(solution)/shard_map/project/pallas_call | solution.py:218
  134.9 4.2 %project.5 = (f32[1024,512]{1,0:T(8,128)S(1)}, f32[512,512]{1,0:T(8,128)S(1)}) custom-call(f32[1024,512]{1,0:T(8,128)S(1)} %get-tuple-element.41.refs_0_, f32[512,512]{1,0:T(8,128)S(1)} %get-tuple-element.42.refs_1_, bf16[4,1536,256]{2,1,0:T(8,128)(2,1)S(1)} %collective-permute-done.6.refs_2_.refs_1_, ...), custom_call_target="tpu_custom_call" | custom-call | flops 3221225472 | bytes 6291456 | tf_op jit(solution)/shard_map/project/pallas_call | solution.py:218
  143.4 3.3 %project.6 = (f32[1024,512]{1,0:T(8,128)S(1)}, f32[4,128,128]{2,1,0:T(8,128)S(1)}) custom-call(f32[1024,512]{1,0:T(8,128)S(1)} %get-tuple-element.49.refs_0_, bf16[4,1024,256]{2,1,0:T(8,128)(2,1)S(1)} %collective-permute-done.8.refs_1_, bf16[4,1024,256]{2,1,0:T(8,128)(2,1)} %copy-done.15, bf16[4,256,512]{2,1,0:T(8,128)(2,1)S(1)} %get-tuple-element.44.refs_3_, ...), custom_call_target="tpu_custom_call" | custom-call | flops 2147483648 | bytes 4194304 | tf_op jit(solution)/shard_map/project/pallas_call | solution.py:218
  146.7 3.0 %collective-permute-start.12 = (bf16[4,128,128]{2,1,0:T(8,128)(2,1)S(1)}, bf16[4,128,128]{2,1,0:T(8,128)(2,1)S(1)}, u32[]{:S(2)}, u32[]{:S(2)}) collective-permute-start(bf16[4,128,128]{2,1,0:T(8,128)(2,1)S(1)} %convert_element_type.136), channel_id=1, source_target_pairs={{0,8},{8,0},{16,24},{24,16},{1,9},{9,1},{17,25},{25,17},{2,10},{10... | collective-permute-start | bytes 393224 | tf_op jit(solution)/shard_map/ppermute | solution.py:29
  154.1 5.1 %collective-permute-done.13 = bf16[4,128,128]{2,1,0:T(8,128)(2,1)S(1)} collective-permute-done((bf16[4,128,128]{2,1,0:T(8,128)(2,1)S(1)}, bf16[4,128,128]{2,1,0:T(8,128)(2,1)S(1)}, u32[]{:S(2)}, u32[]{:S(2)}) %collective-permute-start.13) | collective-permute-done | bytes 131104 | tf_op jit(solution)/shard_map/ppermute | solution.py:29
  166.5 2.7 project.7.pre_q
  171.0 3.3 %attend.1 = (f32[4,128,128]{2,1,0:T(8,128)S(1)}, bf16[512,512]{1,0:T(8,128)(2,1)S(1)}) custom-call(f32[512,512]{1,0:T(8,128)S(1)} %project.7.pre_q, f32[1024,512]{1,0:T(8,128)S(1)} %get-tuple-element.50.pre_k.pre_v.pre_kv, f32[1024,512]{1,0:T(8,128)S(1)} %get-tuple-element.50.pre_k.pre_v.pre_kv, f32[4,128,128]{2,1,0:T(8,128)S(1)} %fusion.2.before, ...), custom_call_target="tpu_custom_call" | custom-call | tf_op jit(solution)/shard_map/attend/pallas_call | solution.py:281
  174.4 2.6 collective-permute-start.19
  178.7 3.8 %attend_back.1 = (bf16[512,512]{1,0:T(8,128)(2,1)S(1)}, f32[512,512]{1,0:T(8,128)S(1)}, f32[512,512]{1,0:T(8,128)S(1)}) custom-call(f32[512,512]{1,0:T(8,128)S(1)} %project.7.pre_q, f32[1024,512]{1,0:T(8,128)S(1)} %get-tuple-element.50.pre_k.pre_v.pre_kv, f32[1024,512]{1,0:T(8,128)S(1)} %get-tuple-element.50.pre_k.pre_v.pre_kv, ...), custom_call_target="tpu_custom_call" | custom-call | flops 805306368 | bytes 4194304 | tf_op jit(solution)/shard_map/attend_back/pallas_call | solution.py:299
  188.6 3.9 %collective-permute-done.23 = bf16[4,128,128]{2,1,0:T(8,128)(2,1)} collective-permute-done((bf16[4,128,128]{2,1,0:T(8,128)(2,1)}, bf16[4,128,128]{2,1,0:T(8,128)(2,1)}, u32[]{:S(2)}, u32[]{:S(2)}) %collective-permute-start.23) | collective-permute-done | bytes 131104 | tf_op jit(solution)/shard_map/ppermute | solution.py:29
  201.7 8.0 %push.4 = (bf16[256,2048]{1,0:T(8,128)(2,1)}, bf16[256,2048]{1,0:T(8,128)(2,1)}) custom-call(bf16[512,1536]{1,0:T(8,128)(2,1)} %copy-done.14, bf16[4,1536,256]{2,1,0:T(8,128)(2,1)} %pad_maximum_fusion.refs_0_, bf16[4,1024,256]{2,1,0:T(8,128)(2,1)} %copy-done.3, bf16[4,512,256]{2,1,0:T(8,128)(2,1)} %collective-permute-done.10.refs_1_.refs_2_), custom_call_target="tpu_custom_call" | custom-call | flops 3221225472 | bytes 6291456 | tf_op jit(solution)/shard_map/push/pallas_call | solution.py:403
  209.8 7.8 %push.6 = (bf16[256,2048]{1,0:T(8,128)(2,1)}, bf16[256,2048]{1,0:T(8,128)(2,1)}) custom-call(bf16[512,1536]{1,0:T(8,128)(2,1)} %copy-done.13, bf16[4,1536,256]{2,1,0:T(8,128)(2,1)} %collective-permute-done.2.refs_1_.refs_0_, bf16[4,1536,256]{2,1,0:T(8,128)(2,1)} %copy-done.12), custom_call_target="tpu_custom_call" | custom-call | flops 3221225472 | bytes 6291456 | tf_op jit(solution)/shard_map/push/pallas_call | solution.py:403
  221.8 2.9 %collective-permute-start.30 = (bf16[128,2048]{1,0:T(8,128)(2,1)S(1)}, bf16[128,2048]{1,0:T(8,128)(2,1)S(1)}, u32[]{:S(2)}, u32[]{:S(2)}) collective-permute-start(bf16[128,2048]{1,0:T(8,128)(2,1)S(1)} %add_convert_fusion.1), channel_id=1, source_target_pairs={{0,6},{2,4},{4,2},{6,0},{1,7},{3,5},{5,3},{7,1},{8,14},{10,12},{12... | collective-permute-start | bytes 1572872 | tf_op jit(solution)/shard_map/ppermute | solution.py:29
  224.6 8.0 %push.5 = (bf16[256,2048]{1,0:T(8,128)(2,1)}, bf16[256,2048]{1,0:T(8,128)(2,1)}) custom-call(bf16[512,1536]{1,0:T(8,128)(2,1)} %copy-done.14, bf16[4,1536,256]{2,1,0:T(8,128)(2,1)} %pad_maximum_fusion.1.refs_2_.refs_0_, bf16[4,1024,256]{2,1,0:T(8,128)(2,1)} %copy-done.15, bf16[4,512,256]{2,1,0:T(8,128)(2,1)} %collective-permute-done.11.refs_2_), custom_call_target="tpu_custom_call" | custom-call | flops 3221225472 | bytes 6291456 | tf_op jit(solution)/shard_map/push/pallas_call | solution.py:403
  233.1 7.6 %push.7 = (bf16[256,2048]{1,0:T(8,128)(2,1)}, bf16[256,2048]{1,0:T(8,128)(2,1)}) custom-call(bf16[512,1536]{1,0:T(8,128)(2,1)} %copy-done.13, bf16[4,1536,256]{2,1,0:T(8,128)(2,1)} %collective-permute-done.5.refs_3_.refs_0_, bf16[4,1536,256]{2,1,0:T(8,128)(2,1)} %copy-done.11), custom_call_target="tpu_custom_call" | custom-call | flops 3221225472 | bytes 6291456 | tf_op jit(solution)/shard_map/push/pallas_call | solution.py:403
  244.8 2.8 %collective-permute-start.34 = (bf16[128,2048]{1,0:T(8,128)(2,1)S(1)}, bf16[128,2048]{1,0:T(8,128)(2,1)S(1)}, u32[]{:S(2)}, u32[]{:S(2)}) collective-permute-start(bf16[128,2048]{1,0:T(8,128)(2,1)S(1)} %add_convert_fusion), channel_id=1, source_target_pairs={{0,6},{2,4},{4,2},{6,0},{1,7},{3,5},{5,3},{7,1},{8,14},{10,12},{12... | collective-permute-start | bytes 1572872 | tf_op jit(solution)/shard_map/ppermute | solution.py:29
  247.7 4.3 %collective-permute-done.26 = bf16[64,2048]{1,0:T(8,128)(2,1)S(1)} collective-permute-done((bf16[64,2048]{1,0:T(8,128)(2,1)S(1)}, bf16[64,2048]{1,0:T(8,128)(2,1)S(1)}, u32[]{:S(2)}, u32[]{:S(2)}) %collective-permute-start.26) | collective-permute-done | bytes 262176 | tf_op jit(solution)/shard_map/ppermute | solution.py:29
  252.1 10.1 %collective-permute-done.32 = bf16[128,2048]{1,0:T(8,128)(2,1)S(1)} collective-permute-done((bf16[128,2048]{1,0:T(8,128)(2,1)S(1)}, bf16[128,2048]{1,0:T(8,128)(2,1)S(1)}, u32[]{:S(2)}, u32[]{:S(2)}) %collective-permute-start.32) | collective-permute-done | bytes 524320 | tf_op jit(solution)/shard_map/ppermute | solution.py:29
  262.4 2.3 collective-permute-start.33
  265.1 6.3 %collective-permute-done.33 = bf16[64,2048]{1,0:T(8,128)(2,1)S(1)} collective-permute-done((bf16[64,2048]{1,0:T(8,128)(2,1)S(1)}, bf16[64,2048]{1,0:T(8,128)(2,1)S(1)}, u32[]{:S(2)}, u32[]{:S(2)}) %collective-permute-start.33) | collective-permute-done | bytes 262176 | tf_op jit(solution)/shard_map/ppermute | solution.py:29
  272.0 2.3 finish.1
  (139 shorter events, 70.8 us)
Async XLA Ops:
  3.0 12.1 %collective-permute-start.3 = (bf16[1,1536,256]{2,1,0:T(8,128)(2,1)S(1)}, bf16[1,1536,256]{2,1,0:T(8,128)(2,1)S(1)}, u32[]{:S(2)}, u32[]{:S(2)}) collective-permute-start(bf16[1,1536,256]{2,1,0:T(8,128)(2,1)S(1)} %get-tuple-element.78), channel_id=1, source_target_pairs={{0,8},{1,25},{8,0},{9,17},{16,24},{17,9},{24,16},{25,1},{32,40},{3... | collective-permute-start | bytes 2359304 | tf_op jit(solution)/shard_map/ppermute | solution.py:40
  4.7 14.7 %collective-permute-start = (bf16[1,1536,256]{2,1,0:T(8,128)(2,1)S(1)}, bf16[1,1536,256]{2,1,0:T(8,128)(2,1)S(1)}, u32[]{:S(2)}, u32[]{:S(2)}) collective-permute-start(bf16[1,1536,256]{2,1,0:T(8,128)(2,1)S(1)} %get-tuple-element.79), channel_id=1, source_target_pairs={{0,32},{1,97},{8,40},{9,105},{16,48},{17,113},{24,56},{25,121},{32... | collective-permute-start | bytes 2359304 | tf_op jit(solution)/shard_map/ppermute | solution.py:40
  16.3 21.9 %collective-permute-start.4 = (bf16[2,1536,256]{2,1,0:T(8,128)(2,1)}, bf16[2,1536,256]{2,1,0:T(8,128)(2,1)}, u32[]{:S(2)}, u32[]{:S(2)}) collective-permute-start(bf16[2,1536,256]{2,1,0:T(8,128)(2,1)} %pad_maximum_fusion.4), channel_id=1, source_target_pairs={{0,24},{1,9},{8,16},{9,1},{16,8},{17,25},{24,0},{25,17},{32,56},{3... | collective-permute-start | bytes 4718600 | tf_op jit(solution)/shard_map/ppermute | solution.py:40
  20.8 22.7 %collective-permute-start.1 = (bf16[2,1536,256]{2,1,0:T(8,128)(2,1)}, bf16[2,1536,256]{2,1,0:T(8,128)(2,1)}, u32[]{:S(2)}, u32[]{:S(2)}) collective-permute-start(bf16[2,1536,256]{2,1,0:T(8,128)(2,1)} %pad_maximum_fusion.3), channel_id=1, source_target_pairs={{0,96},{1,33},{8,104},{9,41},{16,112},{17,49},{24,120},{25,57},{32... | collective-permute-start | bytes 4718600 | tf_op jit(solution)/shard_map/ppermute | solution.py:40
  47.6 59.4 %collective-permute-start.2 = (bf16[4,1536,256]{2,1,0:T(8,128)(2,1)}, bf16[4,1536,256]{2,1,0:T(8,128)(2,1)}, u32[]{:S(2)}, u32[]{:S(2)}) collective-permute-start(bf16[4,1536,256]{2,1,0:T(8,128)(2,1)} %pad_maximum_fusion.refs_0_), channel_id=1, source_target_pairs={{0,8},{1,25},{8,0},{9,17},{16,24},{17,9},{24,16},{25,1},{32,40},{3... | collective-permute-start | bytes 9437192 | tf_op jit(solution)/shard_map/ppermute | solution.py:40
  49.5 60.5 %collective-permute-start.5 = (bf16[4,1536,256]{2,1,0:T(8,128)(2,1)}, bf16[4,1536,256]{2,1,0:T(8,128)(2,1)}, u32[]{:S(2)}, u32[]{:S(2)}) collective-permute-start(bf16[4,1536,256]{2,1,0:T(8,128)(2,1)} %pad_maximum_fusion.1.refs_2_.refs_0_), channel_id=1, source_target_pairs={{0,32},{1,97},{8,40},{9,105},{16,48},{17,113},{24,56},{25,121},{32... | collective-permute-start | bytes 9437192 | tf_op jit(solution)/shard_map/ppermute | solution.py:40
  59.9 64.7 %collective-permute-start.6 = (bf16[4,1536,256]{2,1,0:T(8,128)(2,1)}, bf16[4,1536,256]{2,1,0:T(8,128)(2,1)S(1)}, u32[]{:S(2)}, u32[]{:S(2)}) collective-permute-start(bf16[4,1536,256]{2,1,0:T(8,128)(2,1)} %pad_maximum_fusion.refs_0_), channel_id=1, source_target_pairs={{0,24},{1,9},{8,16},{9,1},{16,8},{17,25},{24,0},{25,17},{32,56},{3... | collective-permute-start | bytes 9437192 | tf_op jit(solution)/shard_map/ppermute | solution.py:40
  61.0 73.8 %collective-permute-start.7 = (bf16[4,1536,256]{2,1,0:T(8,128)(2,1)}, bf16[4,1536,256]{2,1,0:T(8,128)(2,1)S(1)}, u32[]{:S(2)}, u32[]{:S(2)}) collective-permute-start(bf16[4,1536,256]{2,1,0:T(8,128)(2,1)} %pad_maximum_fusion.1.refs_2_.refs_0_), channel_id=1, source_target_pairs={{0,96},{1,33},{8,104},{9,41},{16,112},{17,49},{24,120},{25,57},{32... | collective-permute-start | bytes 9437192 | tf_op jit(solution)/shard_map/ppermute | solution.py:40
  108.7 31.4 %collective-permute-start.8 = (bf16[4,1024,256]{2,1,0:T(8,128)(2,1)S(1)}, bf16[4,1024,256]{2,1,0:T(8,128)(2,1)S(1)}, u32[]{:S(2)}, u32[]{:S(2)}) collective-permute-start(bf16[4,1024,256]{2,1,0:T(8,128)(2,1)S(1)} %slice.148), channel_id=1, source_target_pairs={{0,24},{1,9},{8,16},{9,1},{16,8},{17,25},{24,0},{25,17},{32,56},{3... | collective-permute-start | bytes 6291464 | tf_op jit(solution)/shard_map/ppermute | solution.py:40
  111.8 30.3 %collective-permute-start.9 = (bf16[4,1024,256]{2,1,0:T(8,128)(2,1)S(1)}, bf16[4,1024,256]{2,1,0:T(8,128)(2,1)S(1)}, u32[]{:S(2)}, u32[]{:S(2)}) collective-permute-start(bf16[4,1024,256]{2,1,0:T(8,128)(2,1)S(1)} %slice.149), channel_id=1, source_target_pairs={{0,96},{1,33},{8,104},{9,41},{16,112},{17,49},{24,120},{25,57},{32... | collective-permute-start | bytes 6291464 | tf_op jit(solution)/shard_map/ppermute | solution.py:40
  120.3 43.7 %collective-permute-start.10 = (bf16[4,512,256]{2,1,0:T(8,128)(2,1)}, bf16[4,512,256]{2,1,0:T(8,128)(2,1)}, u32[]{:S(2)}, u32[]{:S(2)}) collective-permute-start(bf16[4,512,256]{2,1,0:T(8,128)(2,1)} %slice.150), channel_id=1, source_target_pairs={{0,24},{1,9},{8,16},{9,1},{16,8},{17,25},{24,0},{25,17},{32,56},{3... | collective-permute-start | bytes 3145736 | tf_op jit(solution)/shard_map/ppermute | solution.py:40
  124.6 39.4 %collective-permute-start.11 = (bf16[4,512,256]{2,1,0:T(8,128)(2,1)}, bf16[4,512,256]{2,1,0:T(8,128)(2,1)}, u32[]{:S(2)}, u32[]{:S(2)}) collective-permute-start(bf16[4,512,256]{2,1,0:T(8,128)(2,1)} %slice.151), channel_id=1, source_target_pairs={{0,96},{1,33},{8,104},{9,41},{16,112},{17,49},{24,120},{25,57},{32... | collective-permute-start | bytes 3145736 | tf_op jit(solution)/shard_map/ppermute | solution.py:40
  146.7 7.4 %collective-permute-start.12 = (bf16[4,128,128]{2,1,0:T(8,128)(2,1)S(1)}, bf16[4,128,128]{2,1,0:T(8,128)(2,1)S(1)}, u32[]{:S(2)}, u32[]{:S(2)}) collective-permute-start(bf16[4,128,128]{2,1,0:T(8,128)(2,1)S(1)} %convert_element_type.136), channel_id=1, source_target_pairs={{0,8},{8,0},{16,24},{24,16},{1,9},{9,1},{17,25},{25,17},{2,10},{10... | collective-permute-start | bytes 393224 | tf_op jit(solution)/shard_map/ppermute | solution.py:29
  149.7 9.5 %collective-permute-start.13 = (bf16[4,128,128]{2,1,0:T(8,128)(2,1)S(1)}, bf16[4,128,128]{2,1,0:T(8,128)(2,1)S(1)}, u32[]{:S(2)}, u32[]{:S(2)}) collective-permute-start(bf16[4,128,128]{2,1,0:T(8,128)(2,1)S(1)} %convert_element_type.136), channel_id=1, source_target_pairs={{0,24},{8,16},{16,8},{24,0},{1,25},{9,17},{17,9},{25,1},{2,26},{10... | collective-permute-start | bytes 393224 | tf_op jit(solution)/shard_map/ppermute | solution.py:29
  149.7 9.5 %collective-permute-start.14 = (bf16[4,128,128]{2,1,0:T(8,128)(2,1)S(1)}, bf16[4,128,128]{2,1,0:T(8,128)(2,1)S(1)}, u32[]{:S(2)}, u32[]{:S(2)}) collective-permute-start(bf16[4,128,128]{2,1,0:T(8,128)(2,1)S(1)} %convert_element_type.136), channel_id=1, source_target_pairs={{0,16},{8,24},{16,0},{24,8},{1,17},{9,25},{17,1},{25,9},{2,18},{10... | collective-permute-start | bytes 393224 | tf_op jit(solution)/shard_map/ppermute | solution.py:29
  159.9 9.3 %collective-permute-start.17 = (bf16[4,128,128]{2,1,0:T(8,128)(2,1)}, bf16[4,128,128]{2,1,0:T(8,128)(2,1)}, u32[]{:S(2)}, u32[]{:S(2)}) collective-permute-start(bf16[4,128,128]{2,1,0:T(8,128)(2,1)} %fusion.3), channel_id=1, source_target_pairs={{0,64},{32,96},{64,0},{96,32},{1,65},{33,97},{65,1},{97,33},{2,66}... | collective-permute-start | bytes 393224 | tf_op jit(solution)/shard_map/ppermute | solution.py:29
  161.3 8.2 %collective-permute-start.16 = (bf16[4,128,128]{2,1,0:T(8,128)(2,1)}, bf16[4,128,128]{2,1,0:T(8,128)(2,1)}, u32[]{:S(2)}, u32[]{:S(2)}) collective-permute-start(bf16[4,128,128]{2,1,0:T(8,128)(2,1)} %fusion.3), channel_id=1, source_target_pairs={{0,96},{32,64},{64,32},{96,0},{1,97},{33,65},{65,33},{97,1},{2,98}... | collective-permute-start | bytes 393224 | tf_op jit(solution)/shard_map/ppermute | solution.py:29
  174.3 10.0 %collective-permute-start.18 = (bf16[4,128,128]{2,1,0:T(8,128)(2,1)S(1)}, bf16[4,128,128]{2,1,0:T(8,128)(2,1)S(1)}, u32[]{:S(2)}, u32[]{:S(2)}) collective-permute-start(bf16[4,128,128]{2,1,0:T(8,128)(2,1)S(1)} %convert_element_type.144), channel_id=1, source_target_pairs={{0,8},{8,0},{16,24},{24,16},{1,9},{9,1},{17,25},{25,17},{2,10},{10... | collective-permute-start | bytes 393224 | tf_op jit(solution)/shard_map/ppermute | solution.py:29
  174.4 9.9 %collective-permute-start.19 = (bf16[4,128,128]{2,1,0:T(8,128)(2,1)S(1)}, bf16[4,128,128]{2,1,0:T(8,128)(2,1)S(1)}, u32[]{:S(2)}, u32[]{:S(2)}) collective-permute-start(bf16[4,128,128]{2,1,0:T(8,128)(2,1)S(1)} %convert_element_type.144), channel_id=1, source_target_pairs={{0,24},{8,16},{16,8},{24,0},{1,25},{9,17},{17,9},{25,1},{2,26},{10... | collective-permute-start | bytes 393224 | tf_op jit(solution)/shard_map/ppermute | solution.py:29
  177.0 7.3 %collective-permute-start.20 = (bf16[4,128,128]{2,1,0:T(8,128)(2,1)S(1)}, bf16[4,128,128]{2,1,0:T(8,128)(2,1)S(1)}, u32[]{:S(2)}, u32[]{:S(2)}) collective-permute-start(bf16[4,128,128]{2,1,0:T(8,128)(2,1)S(1)} %convert_element_type.144), channel_id=1, source_target_pairs={{0,16},{8,24},{16,0},{24,8},{1,17},{9,25},{17,1},{25,9},{2,18},{10... | collective-permute-start | bytes 393224 | tf_op jit(solution)/shard_map/ppermute | solution.py:29
  185.0 7.5 %collective-permute-start.23 = (bf16[4,128,128]{2,1,0:T(8,128)(2,1)}, bf16[4,128,128]{2,1,0:T(8,128)(2,1)}, u32[]{:S(2)}, u32[]{:S(2)}) collective-permute-start(bf16[4,128,128]{2,1,0:T(8,128)(2,1)} %convert_add_fusion.4), channel_id=1, source_target_pairs={{0,64},{32,96},{64,0},{96,32},{1,65},{33,97},{65,1},{97,33},{2,66}... | collective-permute-start | bytes 393224 | tf_op jit(solution)/shard_map/ppermute | solution.py:29
  186.9 7.2 %collective-permute-start.22 = (bf16[4,128,128]{2,1,0:T(8,128)(2,1)}, bf16[4,128,128]{2,1,0:T(8,128)(2,1)}, u32[]{:S(2)}, u32[]{:S(2)}) collective-permute-start(bf16[4,128,128]{2,1,0:T(8,128)(2,1)} %convert_add_fusion.4), channel_id=1, source_target_pairs={{0,96},{32,64},{64,32},{96,0},{1,97},{33,65},{65,33},{97,1},{2,98}... | collective-permute-start | bytes 393224 | tf_op jit(solution)/shard_map/ppermute | solution.py:29
  209.7 8.5 %collective-permute-start.24 = (bf16[256,2048]{1,0:T(8,128)(2,1)}, bf16[256,2048]{1,0:T(8,128)(2,1)S(1)}, u32[]{:S(2)}, u32[]{:S(2)}) collective-permute-start(bf16[256,2048]{1,0:T(8,128)(2,1)} %get-tuple-element.61), channel_id=1, source_target_pairs={{0,1},{1,0},{2,3},{3,2},{4,5},{5,4},{6,7},{7,6},{8,9},{9,8},{10,11... | collective-permute-start | bytes 3145736 | tf_op jit(solution)/shard_map/ppermute | solution.py:29
  218.3 22.9 %collective-permute-start.25 = (bf16[128,2048]{1,0:T(8,128)(2,1)S(1)}, bf16[128,2048]{1,0:T(8,128)(2,1)S(1)}, u32[]{:S(2)}, u32[]{:S(2)}) collective-permute-start(bf16[128,2048]{1,0:T(8,128)(2,1)S(1)} %add_convert_fusion.3), channel_id=1, source_target_pairs={{0,2},{2,0},{4,6},{6,4},{1,3},{3,1},{5,7},{7,5},{8,10},{10,8},{12,... | collective-permute-start | bytes 1572872 | tf_op jit(solution)/shard_map/ppermute | solution.py:29
  221.8 20.3 %collective-permute-start.30 = (bf16[128,2048]{1,0:T(8,128)(2,1)S(1)}, bf16[128,2048]{1,0:T(8,128)(2,1)S(1)}, u32[]{:S(2)}, u32[]{:S(2)}) collective-permute-start(bf16[128,2048]{1,0:T(8,128)(2,1)S(1)} %add_convert_fusion.1), channel_id=1, source_target_pairs={{0,6},{2,4},{4,2},{6,0},{1,7},{3,5},{5,3},{7,1},{8,14},{10,12},{12... | collective-permute-start | bytes 1572872 | tf_op jit(solution)/shard_map/ppermute | solution.py:29
  232.7 10.1 %collective-permute-start.27 = (bf16[256,2048]{1,0:T(8,128)(2,1)}, bf16[256,2048]{1,0:T(8,128)(2,1)S(1)}, u32[]{:S(2)}, u32[]{:S(2)}) collective-permute-start(bf16[256,2048]{1,0:T(8,128)(2,1)} %get-tuple-element.64), channel_id=1, source_target_pairs={{0,1},{1,0},{2,3},{3,2},{4,5},{5,4},{6,7},{7,6},{8,9},{9,8},{10,11... | collective-permute-start | bytes 3145736 | tf_op jit(solution)/shard_map/ppermute | solution.py:29
  241.5 10.5 %collective-permute-start.26 = (bf16[64,2048]{1,0:T(8,128)(2,1)S(1)}, bf16[64,2048]{1,0:T(8,128)(2,1)S(1)}, u32[]{:S(2)}, u32[]{:S(2)}) collective-permute-start(bf16[64,2048]{1,0:T(8,128)(2,1)S(1)} %slice.199), channel_id=1, source_target_pairs={{0,6},{2,4},{4,2},{6,0},{1,7},{3,5},{5,3},{7,1},{8,14},{10,12},{12... | collective-permute-start | bytes 786440 | tf_op jit(solution)/shard_map/ppermute | solution.py:29
  242.4 9.7 %collective-permute-start.31 = (bf16[64,2048]{1,0:T(8,128)(2,1)S(1)}, bf16[64,2048]{1,0:T(8,128)(2,1)S(1)}, u32[]{:S(2)}, u32[]{:S(2)}) collective-permute-start(bf16[64,2048]{1,0:T(8,128)(2,1)S(1)} %slice.198), channel_id=1, source_target_pairs={{0,2},{2,0},{4,6},{6,4},{1,3},{3,1},{5,7},{7,5},{8,10},{10,8},{12,... | collective-permute-start | bytes 786440 | tf_op jit(solution)/shard_map/ppermute | solution.py:29
  242.9 19.3 %collective-permute-start.32 = (bf16[128,2048]{1,0:T(8,128)(2,1)S(1)}, bf16[128,2048]{1,0:T(8,128)(2,1)S(1)}, u32[]{:S(2)}, u32[]{:S(2)}) collective-permute-start(bf16[128,2048]{1,0:T(8,128)(2,1)S(1)} %add_convert_fusion.2), channel_id=1, source_target_pairs={{0,2},{2,0},{4,6},{6,4},{1,3},{3,1},{5,7},{7,5},{8,10},{10,8},{12,... | collective-permute-start | bytes 1572872 | tf_op jit(solution)/shard_map/ppermute | solution.py:29
  244.8 19.9 %collective-permute-start.34 = (bf16[128,2048]{1,0:T(8,128)(2,1)S(1)}, bf16[128,2048]{1,0:T(8,128)(2,1)S(1)}, u32[]{:S(2)}, u32[]{:S(2)}) collective-permute-start(bf16[128,2048]{1,0:T(8,128)(2,1)S(1)} %add_convert_fusion), channel_id=1, source_target_pairs={{0,6},{2,4},{4,2},{6,0},{1,7},{3,5},{5,3},{7,1},{8,14},{10,12},{12... | collective-permute-start | bytes 1572872 | tf_op jit(solution)/shard_map/ppermute | solution.py:29
  262.4 9.0 %collective-permute-start.33 = (bf16[64,2048]{1,0:T(8,128)(2,1)S(1)}, bf16[64,2048]{1,0:T(8,128)(2,1)S(1)}, u32[]{:S(2)}, u32[]{:S(2)}) collective-permute-start(bf16[64,2048]{1,0:T(8,128)(2,1)S(1)} %slice.197), channel_id=1, source_target_pairs={{0,6},{2,4},{4,2},{6,0},{1,7},{3,5},{5,3},{7,1},{8,14},{10,12},{12... | collective-permute-start | bytes 786440 | tf_op jit(solution)/shard_map/ppermute | solution.py:29
  265.0 6.9 %collective-permute-start.35 = (bf16[64,2048]{1,0:T(8,128)(2,1)S(1)}, bf16[64,2048]{1,0:T(8,128)(2,1)S(1)}, u32[]{:S(2)}, u32[]{:S(2)}) collective-permute-start(bf16[64,2048]{1,0:T(8,128)(2,1)S(1)} %slice.196), channel_id=1, source_target_pairs={{0,2},{2,0},{4,6},{6,4},{1,3},{3,1},{5,7},{7,5},{8,10},{10,8},{12,... | collective-permute-start | bytes 786440 | tf_op jit(solution)/shard_map/ppermute | solution.py:29
  (25 other events, 160.0 us)
where the time goes:
time: 280 us; the launch traced here: 275 us
  waiting for transfers between devices  108 us (39%)
  Pallas kernels  69.3 us (25%)
  starting transfers between devices  54.8 us (20%)
  local copies, waits for them, and re-layouts  26.3 us (9%)
  other arithmetic  15 us (5%)
    ppermute x12, waiting for transfers between devices, swap_links(): return lax.ppermute(x, ('z', 'y', 'c'), pairs)  73 us
    ppermute x24, waiting for transfers between devices, swap(): return lax.ppermute(x, axis, [(i, i ^ offset) for i in range(n)])  35.4 us
    pallas_call x4, Pallas kernels, push(): pl.pallas_call(functools.partial(push_kernel, kind), in_specs=[hbm] * (1...  31.4 us
    ppermute x24, starting transfers between devices, swap(): return lax.ppermute(x, axis, [(i, i ^ offset) for i in range(n)])  31 us
    ppermute x12, starting transfers between devices, swap_links(): return lax.ppermute(x, ('z', 'y', 'c'), pairs)  23.8 us
    pallas_call x4, Pallas kernels, project(): pl.pallas_call(functools.partial(project_kernel, slots, len(start), heads...  20.3 us
    unnamed x42, local copies, waits for them, and re-layouts  14.6 us
    pallas_call x1, Pallas kernels, reorder_columns(): pl.pallas_call(reorder_kernel, grid_spec=pltpu.PrefetchScalarGridSpec(num...  6.48 us
  transfers between devices with their start and end apart: 36, of which 17 were waited for; matrix products, arithmetic and copies ran while one was open for 6% of the time, Pallas kernels for 20%

commit v1 on v0

--- a/solution.py
+++ b/solution.py
@@ -312,12 +312,64 @@
     )(pre_query, pre_kv, pre_kv, before, grad_att)
 
 
-def row_order(first):
-    second = 4 - first
-    return [(ox, oc) for oc in (1, 0) for ox in (0, second, first, 2)]
-
-
-def collect_kernel(table, pre_kv, grad_k, grad_v, back_q, later, rows1, rows3, back):
+def row_table():
+    x, c = lax.axis_index("x"), lax.axis_index("c")
+    groups = []
+    for oc in (1, 0):
+        owner = c ^ oc
+        for ox0, ox1 in ((0, 0), (3, 1), (1, 3), (2, 2)):
+            groups.append((x ^ jnp.where(owner == 0, ox0, ox1)) * 2 + owner)
+    return jnp.stack(groups).astype(jnp.int32)
+
+
+def swap_rings(a, step):
+    pairs = []
+    for x in range(4):
+        for c in range(2):
+            pairs.append((x * 2 + c, (x ^ ((1, 3), (3, 1))[step][c]) * 2 + c))
+    return lax.ppermute(a, ("x", "c"), pairs)
+
+
+def chunk_copies(kind, srcs, bufs, sems):
+    sides = [[(srcs[0], bufs[0])], [(src, buf) for src, buf in zip(srcs[1:], bufs[1:])]]
+    pairs = []
+    for i in range(4):
+        at = pl.ds(2 * (i % 2), 2)
+        pairs.append([pltpu.make_async_copy(s.at[at], b.at[at], sems.at[2 * i + j]) for j, (s, b) in enumerate(sides[i // 2])])
+    return sides, pairs
+
+
+def push_chunk(kind, rows, sides, pairs, outs, out_bufs, out_sems):
+    half = rows.shape[0] // 2
+    c = lax.axis_index("c")
+    places = (c, 1 - c) if kind else (0, 1)
+    leaving = []
+    for i in range(4):
+        for copy in pairs[i]:
+            copy.wait()
+        total, at = None, 0
+        for _, buf in sides[i // 2]:
+            side = jnp.concatenate([buf[2 * (i % 2)], buf[2 * (i % 2) + 1]], axis=1)
+            term = dot(rows[:, at : at + side.shape[0]], side)
+            total = term if total is None else total + term
+            at += side.shape[0]
+        cols = pl.ds(pl.multiple_of(places[i // 2] * 1024 + (i % 2) * 512, 512), 512)
+        for j, part in enumerate((total[:half], total[half:])):
+            out_bufs[j][i] = part.astype(out_bufs[j].dtype)
+            leaving.append(pltpu.make_async_copy(out_bufs[j].at[i], outs[j].at[:, cols], out_sems.at[2 * i + j]))
+            leaving[-1].start()
+    return leaving
+
+
+def collect_kernel(count, table, pre_kv, grad_k, grad_v, back_q, later, *refs):
+    srcs, (rows_out, other, mine) = refs[:count], refs[count : count + 3]
+    back = refs[count + 3]
+    bufs = refs[count + 4 : 2 * count + 4]
+    other_buf, mine_buf, sems, out_sems, rows, rows_sem = refs[2 * count + 4 :]
+    sides, pairs = chunk_copies(0, srcs, bufs, sems)
+    for pair in pairs:
+        for copy in pair:
+            copy.start()
     width, n = back_q.shape
     for h in range(width // DH):
         cols = slice(h * DH, (h + 1) * DH)
@@ -331,93 +383,91 @@
         back[:, vcols] = (grad_v[cols, :] + dot(a, k, TN)).astype(BF).T
         back[:, qcols] = back_q[cols, :].T
     g = n // 8
-    for f, rows in enumerate((rows1, rows3)):
-        for k in range(8):
-            rows[k * g : (k + 1) * g, :] = back[pl.ds(pl.multiple_of(table[f * 8 + k] * g, g), g), :]
-
-
-def collect(pre_kv, grad_k, grad_v, back_q, later):
+    for k in range(8):
+        rows[k * g : (k + 1) * g, :] = back[pl.ds(pl.multiple_of(table[k] * g, g), g), :]
+    leaving = [pltpu.make_async_copy(rows, rows_out, rows_sem)]
+    leaving[0].start()
+    leaving += push_chunk(0, rows, sides, pairs, (other, mine), (other_buf, mine_buf), out_sems)
+    for copy in leaving:
+        copy.wait()
+
+
+def out_scratch(n):
+    return [
+        pltpu.VMEM((4, n // 2, 512), BF),
+        pltpu.VMEM((4, n // 2, 512), BF),
+        pltpu.SemaphoreType.DMA((8,)),
+        pltpu.SemaphoreType.DMA((8,)),
+    ]
+
+
+def collect(pre_kv, grad_k, grad_v, back_q, later, weights):
     width, n = back_q.shape
-    x, c = lax.axis_index("x"), lax.axis_index("c")
-    table = jnp.stack([(x ^ ox) * 2 + (c ^ oc) for first in (1, 3) for ox, oc in row_order(first)]).astype(jnp.int32)
-    return pl.pallas_call(
-        collect_kernel,
-        in_specs=[pl.BlockSpec(memory_space=pltpu.SMEM)] + [pl.BlockSpec(memory_space=pltpu.VMEM)] * 5,
-        out_specs=[pl.BlockSpec(memory_space=pltpu.VMEM)] * 2,
-        out_shape=[jax.ShapeDtypeStruct((n, 3 * width), BF)] * 2,
-        scratch_shapes=[pltpu.VMEM((n, 3 * width), BF)],
-        compiler_params=pltpu.CompilerParams(vmem_limit_bytes=8 << 20),
-        name="collect",
-    )(table, pre_kv, grad_k, grad_v, back_q, later)
-
-
-def push_kernel(kind, rows_in, *refs):
-    count = 2 if kind else 3
-    other, mine = refs[count : count + 2]
-    rows = refs[count + 2]
-    bufs = refs[count + 3 : 2 * count + 3]
-    other_buf, mine_buf, sems, out_sems, rows_sem = refs[2 * count + 3 :]
-    half = other.shape[0]
-    c = lax.axis_index("c")
-    places = (c, 1 - c) if kind else (0, 1)
-    take_rows = pltpu.make_async_copy(rows_in, rows, rows_sem)
-    take_rows.start()
-    sides = [[(refs[0], bufs[0], 0)], [(refs[1], bufs[1], 0)]]
-    if not kind:
-        sides[1].append((refs[2], bufs[2], refs[1].shape[1]))
-    copies = []
-    for i in range(4):
-        at = pl.ds(2 * (i % 2), 2)
-        copies.append(
-            [
-                pltpu.make_async_copy(src.at[at], buf.at[at], sems.at[2 * i + j])
-                for j, (src, buf, _) in enumerate(sides[i // 2])
-            ]
-        )
-    for group in copies:
-        for copy in group:
-            copy.start()
-    take_rows.wait()
-    outs = []
-    for i in range(4):
-        for copy in copies[i]:
-            copy.wait()
-        total = None
-        for _, buf, at in sides[i // 2]:
-            side = jnp.concatenate([buf[2 * (i % 2)], buf[2 * (i % 2) + 1]], axis=1)
-            term = dot(rows[:, at : at + side.shape[0]], side)
-            total = term if total is None else total + term
-        other_buf[i] = total[:half].astype(other.dtype)
-        mine_buf[i] = total[half:].astype(mine.dtype)
-        cols = pl.ds(pl.multiple_of(places[i // 2] * 1024 + (i % 2) * 512, 512), 512)
-        for j, (buf, out) in enumerate(((other_buf, other), (mine_buf, mine))):
-            outs.append(pltpu.make_async_copy(buf.at[i], out.at[:, cols], out_sems.at[2 * i + j]))
-            outs[-1].start()
-    for copy in outs:
-        copy.wait()
-
-
-def push(kind, rows, weights):
-    n = rows.shape[0]
+    vmem = pl.BlockSpec(memory_space=pltpu.VMEM)
     hbm = pl.BlockSpec(memory_space=pltpu.HBM)
     return pl.pallas_call(
-        functools.partial(push_kernel, kind),
-        in_specs=[hbm] * (1 + len(weights)),
-        out_specs=[hbm] * 2,
-        out_shape=[jax.ShapeDtypeStruct((n // 2, 2048), BF)] * 2,
+        functools.partial(collect_kernel, len(weights)),
+        in_specs=[pl.BlockSpec(memory_space=pltpu.SMEM)] + [vmem] * 5 + [hbm] * len(weights),
+        out_specs=[hbm] * 3,
+        out_shape=[jax.ShapeDtypeStruct((n, 3 * width), BF)] + [jax.ShapeDtypeStruct((n // 2, 2048), BF)] * 2,
         scratch_shapes=[
-            pltpu.VMEM(rows.shape, BF),
+            pltpu.VMEM((n, 3 * width), BF),
             *(pltpu.VMEM(w.shape, BF) for w in weights),
-            pltpu.VMEM((4, n // 2, 512), BF),
-            pltpu.VMEM((4, n // 2, 512), BF),
-            pltpu.SemaphoreType.DMA((8,)),
-            pltpu.SemaphoreType.DMA((8,)),
+            *out_scratch(n),
+            pltpu.VMEM((n, 3 * width), BF),
             pltpu.SemaphoreType.DMA,
         ],
         cost_estimate=pl.CostEstimate(flops=2 * n * 1536 * 2048, bytes_accessed=1536 * 4096, transcendentals=0),
+        compiler_params=pltpu.CompilerParams(vmem_limit_bytes=30 << 20),
+        name="collect",
+    )(row_table(), pre_kv, grad_k, grad_v, back_q, later, *weights)
+
+
+def push_kernel(kinds, counts, *refs):
+    rows_in, srcs = refs[: len(kinds)], refs[len(kinds) : len(kinds) + sum(counts)]
+    refs = refs[len(kinds) + sum(counts) :]
+    outs, refs = refs[: 2 * len(kinds)], refs[2 * len(kinds) :]
+    work = []
+    for m, kind in enumerate(kinds):
+        at = sum(counts[:m])
+        rows, refs = refs[0], refs[1:]
+        bufs, refs = refs[: counts[m]], refs[counts[m] :]
+        (other_buf, mine_buf, sems, out_sems, rows_sem), refs = refs[:5], refs[5:]
+        take_rows = pltpu.make_async_copy(rows_in[m], rows, rows_sem)
+        take_rows.start()
+        sides, pairs = chunk_copies(kind, srcs[at : at + counts[m]], bufs, sems)
+        for pair in pairs:
+            for copy in pair:
+                copy.start()
+        work.append((take_rows, kind, rows, sides, pairs, outs[2 * m : 2 * m + 2], (other_buf, mine_buf), out_sems))
+    leaving = []
+    for take_rows, *rest in work:
+        take_rows.wait()
+        leaving += push_chunk(*rest)
+    for copy in leaving:
+        copy.wait()
+
+
+def push(share, kinds, rows, weights):
+    n = rows[0].shape[0]
+    hbm = pl.BlockSpec(memory_space=pltpu.HBM)
+    loads = [2 * n * 1536 * 2048 // 100 * share for _ in kinds]
+    counts = tuple(map(len, weights))
+    scratch = []
+    for r, ws in zip(rows, weights):
+        scratch += [pltpu.VMEM(r.shape, BF), *(pltpu.VMEM(w.shape, BF) for w in ws), *out_scratch(n), pltpu.SemaphoreType.DMA]
+    return pl.pallas_call(
+        functools.partial(push_kernel, kinds, counts),
+        in_specs=[hbm] * (len(kinds) + sum(counts)),
+        out_specs=[hbm] * (2 * len(kinds)),
+        out_shape=[jax.ShapeDtypeStruct((n // 2, 2048), BF)] * (2 * len(kinds)),
+        scratch_shapes=scratch,
+        cost_estimate=pl.CostEstimate(
+            flops=int(sum(loads)), bytes_accessed=1, transcendentals=0
+        ),
         compiler_params=pltpu.CompilerParams(vmem_limit_bytes=54 << 20),
         name="push",
-    )(rows, *weights)
+    )(*rows, *(w for ws in weights for w in ws))
 
 
 def transposed(w):
@@ -443,32 +493,36 @@
     inner, total = state_round(own_grad, "y", True)
     outer, _ = state_round(after(total, back_q), "z", True)
     later = inner + outer
-    rows = collect(pre_kv, grad_k, grad_v, back_q, later)
-
+    weights = [w for h in (0, 1) for w in ((held[h], last_kv[h], last_q[h]), (near[h], far[h]))]
+    rows, *chunk = collect(pre_kv, grad_k, grad_v, back_q, later, weights[0])
     size = n // 8
+    started = []
+    for i in range(4):
+        if i:
+            use = rows
+            if i == 2:
+                use = after(rows, started[0][0])
+            if i == 3:
+                use = after(rows, started[1][0], started[0][1][0])
+            chunk = push(100, (i % 2,), (use,), weights[i : i + 1])
+        other, mine = chunk
+        got = swap(other, "c", 1)
+        send = (mine[2 * size :].astype(F32) + got[2 * size :].astype(F32)).astype(BF)
+        got = mine[: 2 * size].astype(F32) + got[: 2 * size].astype(F32)
+        got2 = swap_rings(send, 0)
+        keep = got + got2.astype(F32)
+        started.append((send, (got2, keep[size:].astype(BF)), keep))
     tables = []
-    started = []
     for h in (0, 1):
-        for kind in (0, 1):
-            use = rows[kind]
-            if len(started) >= 2:
-                use = after(use, started[-2][0])
-            other, mine = push(kind, use, (near[h], far[h]) if kind else (held[h], last_kv[h], last_q[h]))
-            got = swap(other, "c", 1)
-            send = (mine[2 * size :].astype(F32) + got[2 * size :].astype(F32)).astype(BF)
-            started.append((send, mine, got, swap(send, "x", (1, 3)[kind])))
-            src = sources(h, 0)
-            picks = (0, 1, 2, 3, 12, 13, 14, 15) if kind == 0 else (4, 5, 6, 7, 8, 9, 10, 11)
+        src = sources(h, 0)
+        for picks in ((0, 1, 2, 3, 12, 13, 14, 15), (4, 5, 6, 7, 8, 9, 10, 11)):
             tables.append(jnp.stack([src[p] for p in picks]))
-    middle = []
-    for i, (send, mine, got, got2) in enumerate(started):
-        keep = mine[: 2 * size].astype(F32) + got[: 2 * size].astype(F32) + got2.astype(F32)
-        middle.append((keep, swap(keep[size:].astype(BF), "x", (3, 1)[i % 2])))
     parts = []
-    for i, (keep, got3) in enumerate(middle):
+    for i, (_, (_, send), keep) in enumerate(started):
+        got = swap_rings(send, 1)
         if i < 2:
-            got3 = after(got3, started[2][0], started[3][0])
-        parts.append(keep[:size] + got3.astype(F32))
+            got = after(got, started[2][0], started[3][0])
+        parts.append(keep[:size] + got.astype(F32))
     return finish(parts, jnp.concatenate(tables).astype(jnp.int32))
 
 

time: 280 us -> 276 us (0.986)
  the two profiles are of different devices: /device:TPU:0 before, /device:TPU:1 now
where the time goes in v1:
time: 276 us; the launch traced here: 270 us
  waiting for transfers between devices  122 us (44%)
  Pallas kernels  66.2 us (24%)
  starting transfers between devices  37.8 us (14%)
  local copies, waits for them, and re-layouts  28.8 us (10%)
  other arithmetic  14.5 us (5%)
    ppermute x12, waiting for transfers between devices, swap_links(): return lax.ppermute(x, ('z', 'y', 'c'), pairs)  85 us
    pallas_call x3, Pallas kernels, push(): pl.pallas_call(functools.partial(push_kernel, kinds, counts), in_specs=[h...  23.3 us
    ppermute x8, waiting for transfers between devices, swap_rings(): return lax.ppermute(a, ('x', 'c'), pairs)  22.2 us
    pallas_call x4, Pallas kernels, project(): pl.pallas_call(functools.partial(project_kernel, slots, len(start), heads...  20.3 us
    unnamed x48, local copies, waits for them, and re-layouts  17.2 us
    ppermute x16, starting transfers between devices, swap(): return lax.ppermute(x, axis, [(i, i ^ offset) for i in range(n)])  15.2 us
    ppermute x16, waiting for transfers between devices, swap(): return lax.ppermute(x, axis, [(i, i ^ offset) for i in range(n)])  14.8 us
    ppermute x12, starting transfers between devices, swap_links(): return lax.ppermute(x, ('z', 'y', 'c'), pairs)  14 us
  transfers between devices with their start and end apart: 36, of which 18 were waited for; matrix products, arithmetic and copies ran while one was open for 7% of the time, Pallas kernels for 20%

profile of v1, /device:TPU:1, one launch (start us, length us, event | category | flops | bytes accessed | tf_op | source)
XLA Modules:
  0.0 270.4 jit_solution(11963517964535553196)
XLA Ops:
  3.0 3.6 %collective-permute-start.3 = (bf16[1,1536,256]{2,1,0:T(8,128)(2,1)S(1)}, bf16[1,1536,256]{2,1,0:T(8,128)(2,1)S(1)}, u32[]{:S(2)}, u32[]{:S(2)}) collective-permute-start(bf16[1,1536,256]{2,1,0:T(8,128)(2,1)S(1)} %get-tuple-element.76), channel_id=1, source_target_pairs={{0,8},{1,25},{8,0},{9,17},{16,24},{17,9},{24,16},{25,1},{32,40},{3... | collective-permute-start | bytes 2359304 | tf_op jit(solution)/shard_map/ppermute | solution.py:40
  6.6 3.8 %collective-permute-start = (bf16[1,1536,256]{2,1,0:T(8,128)(2,1)S(1)}, bf16[1,1536,256]{2,1,0:T(8,128)(2,1)S(1)}, u32[]{:S(2)}, u32[]{:S(2)}) collective-permute-start(bf16[1,1536,256]{2,1,0:T(8,128)(2,1)S(1)} %get-tuple-element.77), channel_id=1, source_target_pairs={{0,32},{1,97},{8,40},{9,105},{16,48},{17,113},{24,56},{25,121},{32... | collective-permute-start | bytes 2359304 | tf_op jit(solution)/shard_map/ppermute | solution.py:40
  10.4 5.6 %collective-permute-done.3 = bf16[1,1536,256]{2,1,0:T(8,128)(2,1)S(1)} collective-permute-done((bf16[1,1536,256]{2,1,0:T(8,128)(2,1)S(1)}, bf16[1,1536,256]{2,1,0:T(8,128)(2,1)S(1)}, u32[]{:S(2)}, u32[]{:S(2)}) %collective-permute-start.3) | collective-permute-done | bytes 786464 | tf_op jit(solution)/shard_map/ppermute | solution.py:40
  21.1 16.1 %collective-permute-done.4 = bf16[2,1536,256]{2,1,0:T(8,128)(2,1)} collective-permute-done((bf16[2,1536,256]{2,1,0:T(8,128)(2,1)}, bf16[2,1536,256]{2,1,0:T(8,128)(2,1)}, u32[]{:S(2)}, u32[]{:S(2)}) %collective-permute-start.4) | collective-permute-done | bytes 1572896 | tf_op jit(solution)/shard_map/ppermute | solution.py:40
  37.2 3.8 %collective-permute-done.1 = bf16[2,1536,256]{2,1,0:T(8,128)(2,1)} collective-permute-done((bf16[2,1536,256]{2,1,0:T(8,128)(2,1)}, bf16[2,1536,256]{2,1,0:T(8,128)(2,1)}, u32[]{:S(2)}, u32[]{:S(2)}) %collective-permute-start.1) | collective-permute-done | bytes 1572896 | tf_op jit(solution)/shard_map/ppermute | solution.py:40
  47.2 3.6 %collective-permute-start.5 = (bf16[4,1536,256]{2,1,0:T(8,128)(2,1)}, bf16[4,1536,256]{2,1,0:T(8,128)(2,1)}, u32[]{:S(2)}, u32[]{:S(2)}) collective-permute-start(bf16[4,1536,256]{2,1,0:T(8,128)(2,1)} %pad_maximum_fusion.1.refs_2_.refs_1_), channel_id=1, source_target_pairs={{0,32},{1,97},{8,40},{9,105},{16,48},{17,113},{24,56},{25,121},{32... | collective-permute-start | bytes 9437192 | tf_op jit(solution)/shard_map/ppermute | solution.py:40
  51.3 3.4 %copy-done = bf16[512,8192]{1,0:T(8,128)(2,1)S(1)} copy-done((bf16[512,8192]{1,0:T(8,128)(2,1)S(1)}, bf16[512,8192]{1,0:T(8,128)(2,1)}, u32[]{:S(2)}) %copy-start) | copy-done | bytes 8388632
  54.7 6.5 %reorder_columns.1 = (bf16[8,256,512]{2,1,0:T(8,128)(2,1)S(1)}, bf16[4,256,512]{2,1,0:T(8,128)(2,1)S(1)}, bf16[4,256,512]{2,1,0:T(8,128)(2,1)S(1)}, bf16[8,256,5...) custom-call(s32[2,16]{1,0:T(2,128)S(1)} %pad_add_fusion.table, ...), custom_call_target="tpu_custom_call" | custom-call | bytes 16777216 | tf_op jit(solution)/shard_map/reorder_columns/pallas_call | solution.py:107
  62.1 37.5 %collective-permute-done.2.refs_1_ = bf16[4,1536,256]{2,1,0:T(8,128)(2,1)} collective-permute-done((bf16[4,1536,256]{2,1,0:T(8,128)(2,1)}, bf16[4,1536,256]{2,1,0:T(8,128)(2,1)}, u32[]{:S(2)}, u32[]{:S(2)}) %collective-permute-start.2) | collective-permute-done | bytes 3145760 | tf_op jit(solution)/shard_map/ppermute | solution.py:40
  101.4 3.4 %collective-permute-done.5.refs_3_.refs_1_ = bf16[4,1536,256]{2,1,0:T(8,128)(2,1)} collective-permute-done((bf16[4,1536,256]{2,1,0:T(8,128)(2,1)}, bf16[4,1536,256]{2,1,0:T(8,128)(2,1)}, u32[]{:S(2)}, u32[]{:S(2)}) %collective-permute-start.5) | collective-permute-done | bytes 3145760 | tf_op jit(solution)/shard_map/ppermute | solution.py:40
  106.6 2.4 slice.150
  112.3 7.4 %collective-permute-done.6.refs_2_ = bf16[4,1536,256]{2,1,0:T(8,128)(2,1)S(1)} collective-permute-done((bf16[4,1536,256]{2,1,0:T(8,128)(2,1)}, bf16[4,1536,256]{2,1,0:T(8,128)(2,1)S(1)}, u32[]{:S(2)}, u32[]{:S(2)}) %collective-permute-start.6) | collective-permute-done | bytes 3145760 | tf_op jit(solution)/shard_map/ppermute | solution.py:40
  119.9 10.1 %project.4 = (f32[1024,512]{1,0:T(8,128)S(1)}, f32[512,512]{1,0:T(8,128)S(1)}) custom-call(bf16[4,1536,256]{2,1,0:T(8,128)(2,1)} %pad_maximum_fusion.refs_0_, bf16[4,1536,256]{2,1,0:T(8,128)(2,1)} %collective-permute-done.2.refs_1_, bf16[4,1536,256]{2,1,0:T(8,128)(2,1)} %pad_maximum_fusion.1.refs_2_.refs_1_, ...), custom_call_target="tpu_custom_call" | custom-call | flops 6442450944 | bytes 12582912 | tf_op jit(solution)/shard_map/project/pallas_call | solution.py:218
  130.0 4.2 %project.5 = (f32[1024,512]{1,0:T(8,128)S(1)}, f32[512,512]{1,0:T(8,128)S(1)}) custom-call(f32[1024,512]{1,0:T(8,128)S(1)} %get-tuple-element.40.refs_0_, f32[512,512]{1,0:T(8,128)S(1)} %get-tuple-element.41.refs_1_, bf16[4,1536,256]{2,1,0:T(8,128)(2,1)S(1)} %collective-permute-done.6.refs_2_, ...), custom_call_target="tpu_custom_call" | custom-call | flops 3221225472 | bytes 6291456 | tf_op jit(solution)/shard_map/project/pallas_call | solution.py:218
  135.2 7.1 %collective-permute-done.8.refs_1_ = bf16[4,1024,256]{2,1,0:T(8,128)(2,1)S(1)} collective-permute-done((bf16[4,1024,256]{2,1,0:T(8,128)(2,1)S(1)}, bf16[4,1024,256]{2,1,0:T(8,128)(2,1)S(1)}, u32[]{:S(2)}, u32[]{:S(2)}) %collective-permute-start.8) | collective-permute-done | bytes 2097184 | tf_op jit(solution)/shard_map/ppermute | solution.py:40
  145.6 3.3 %project.6 = (f32[1024,512]{1,0:T(8,128)S(1)}, f32[4,128,128]{2,1,0:T(8,128)S(1)}) custom-call(f32[1024,512]{1,0:T(8,128)S(1)} %get-tuple-element.48.refs_0_, bf16[4,1024,256]{2,1,0:T(8,128)(2,1)S(1)} %collective-permute-done.8.refs_1_, bf16[4,1024,256]{2,1,0:T(8,128)(2,1)} %copy-done.17, bf16[4,256,512]{2,1,0:T(8,128)(2,1)S(1)} %get-tuple-element.43.refs_3_, ...), custom_call_target="tpu_custom_call" | custom-call | flops 2147483648 | bytes 4194304 | tf_op jit(solution)/shard_map/project/pallas_call | solution.py:218
  152.6 3.7 %collective-permute-done.12 = bf16[4,128,128]{2,1,0:T(8,128)(2,1)S(1)} collective-permute-done((bf16[4,128,128]{2,1,0:T(8,128)(2,1)S(1)}, bf16[4,128,128]{2,1,0:T(8,128)(2,1)S(1)}, u32[]{:S(2)}, u32[]{:S(2)}) %collective-permute-start.12) | collective-permute-done | bytes 131104 | tf_op jit(solution)/shard_map/ppermute | solution.py:29
  156.3 3.1 %collective-permute-done.13 = bf16[4,128,128]{2,1,0:T(8,128)(2,1)S(1)} collective-permute-done((bf16[4,128,128]{2,1,0:T(8,128)(2,1)S(1)}, bf16[4,128,128]{2,1,0:T(8,128)(2,1)S(1)}, u32[]{:S(2)}, u32[]{:S(2)}) %collective-permute-start.13) | collective-permute-done | bytes 131104 | tf_op jit(solution)/shard_map/ppermute | solution.py:29
  166.0 2.7 project.7.pre_q
  171.6 3.3 %attend.1 = (f32[4,128,128]{2,1,0:T(8,128)S(1)}, bf16[512,512]{1,0:T(8,128)(2,1)S(1)}) custom-call(f32[512,512]{1,0:T(8,128)S(1)} %project.7.pre_q, f32[1024,512]{1,0:T(8,128)S(1)} %get-tuple-element.49.pre_k.pre_v.pre_kv, f32[1024,512]{1,0:T(8,128)S(1)} %get-tuple-element.49.pre_k.pre_v.pre_kv, f32[4,128,128]{2,1,0:T(8,128)S(1)} %fusion.2.before, ...), custom_call_target="tpu_custom_call" | custom-call | tf_op jit(solution)/shard_map/attend/pallas_call | solution.py:281
  178.5 3.8 %attend_back.1 = (bf16[512,512]{1,0:T(8,128)(2,1)S(1)}, f32[512,512]{1,0:T(8,128)S(1)}, f32[512,512]{1,0:T(8,128)S(1)}) custom-call(f32[512,512]{1,0:T(8,128)S(1)} %project.7.pre_q, f32[1024,512]{1,0:T(8,128)S(1)} %get-tuple-element.49.pre_k.pre_v.pre_kv, f32[1024,512]{1,0:T(8,128)S(1)} %get-tuple-element.49.pre_k.pre_v.pre_kv, ...), custom_call_target="tpu_custom_call" | custom-call | flops 805306368 | bytes 4194304 | tf_op jit(solution)/shard_map/attend_back/pallas_call | solution.py:299
  187.9 2.6 collective-permute-done.23
  190.5 3.8 %collective-permute-done.22 = bf16[4,128,128]{2,1,0:T(8,128)(2,1)S(1)} collective-permute-done((bf16[4,128,128]{2,1,0:T(8,128)(2,1)S(1)}, bf16[4,128,128]{2,1,0:T(8,128)(2,1)S(1)}, u32[]{:S(2)}, u32[]{:S(2)}) %collective-permute-start.22) | collective-permute-done | bytes 131104 | tf_op jit(solution)/shard_map/ppermute | solution.py:29
  199.5 6.7 %collect.1 = (bf16[512,1536]{1,0:T(8,128)(2,1)S(1)}, bf16[256,2048]{1,0:T(8,128)(2,1)}, bf16[256,2048]{1,0:T(8,128)(2,1)S(1)}) custom-call(s32[8]{0:T(128)S(1)} %stack.308.table, f32[1024,512]{1,0:T(8,128)S(1)} %get-tuple-element.49.pre_k.pre_v.pre_kv, f32[512,512]{1,0:T(8,128)S(1)} %copy-done.11, f32[512,512]{1,0:T(8,128)S(1)} %copy-done.13, ...), custom_call_target="tpu_custom_call" | custom-call | flops 3221225472 | bytes 6291456 | tf_op jit(solution)/shard_map/collect/pallas_call | solution.py:408
  208.7 7.7 %push.4 = (bf16[256,2048]{1,0:T(8,128)(2,1)}, bf16[256,2048]{1,0:T(8,128)(2,1)}) custom-call(bf16[512,1536]{1,0:T(8,128)(2,1)} %copy-done.16, bf16[4,1536,256]{2,1,0:T(8,128)(2,1)} %collective-permute-done.2.refs_1_, bf16[4,1536,256]{2,1,0:T(8,128)(2,1)} %copy-done.9), custom_call_target="tpu_custom_call" | custom-call | flops 3221225472 | bytes 1 | tf_op jit(solution)/shard_map/push/pallas_call | solution.py:459
  217.8 2.6 collective-permute-start.25
  220.4 8.0 %push.3 = (bf16[256,2048]{1,0:T(8,128)(2,1)}, bf16[256,2048]{1,0:T(8,128)(2,1)}) custom-call(bf16[512,1536]{1,0:T(8,128)(2,1)} %copy-done.16, bf16[4,1536,256]{2,1,0:T(8,128)(2,1)} %pad_maximum_fusion.1.refs_2_.refs_1_, bf16[4,1024,256]{2,1,0:T(8,128)(2,1)} %copy-done.17, bf16[4,512,256]{2,1,0:T(8,128)(2,1)} %collective-permute-done.11.refs_2_.refs_3_), custom_call_target="tpu_custom_call" | custom-call | flops 3221225472 | bytes 1 | tf_op jit(solution)/shard_map/push/pallas_call | solution.py:459
  230.3 7.7 %push.5 = (bf16[256,2048]{1,0:T(8,128)(2,1)}, bf16[256,2048]{1,0:T(8,128)(2,1)}) custom-call(bf16[512,1536]{1,0:T(8,128)(2,1)} %copy-done.16, bf16[4,1536,256]{2,1,0:T(8,128)(2,1)} %collective-permute-done.5.refs_3_.refs_1_, bf16[4,1536,256]{2,1,0:T(8,128)(2,1)} %copy-done.8), custom_call_target="tpu_custom_call" | custom-call | flops 3221225472 | bytes 1 | tf_op jit(solution)/shard_map/push/pallas_call | solution.py:459
  245.1 10.3 %collective-permute-done.32 = bf16[128,2048]{1,0:T(8,128)(2,1)S(1)} collective-permute-done((bf16[128,2048]{1,0:T(8,128)(2,1)S(1)}, bf16[128,2048]{1,0:T(8,128)(2,1)S(1)}, u32[]{:S(2)}, u32[]{:S(2)}) %collective-permute-start.32) | collective-permute-done | bytes 524320 | tf_op jit(solution)/shard_map/ppermute | solution.py:330
  255.8 6.2 %collective-permute-done.34 = bf16[128,2048]{1,0:T(8,128)(2,1)S(1)} collective-permute-done((bf16[128,2048]{1,0:T(8,128)(2,1)S(1)}, bf16[128,2048]{1,0:T(8,128)(2,1)S(1)}, u32[]{:S(2)}, u32[]{:S(2)}) %collective-permute-start.34) | collective-permute-done | bytes 524320 | tf_op jit(solution)/shard_map/ppermute | solution.py:330
  263.1 4.5 %collective-permute-done.35 = bf16[64,2048]{1,0:T(8,128)(2,1)S(1)} collective-permute-done((bf16[64,2048]{1,0:T(8,128)(2,1)S(1)}, bf16[64,2048]{1,0:T(8,128)(2,1)S(1)}, u32[]{:S(2)}, u32[]{:S(2)}) %collective-permute-start.35) | collective-permute-done | bytes 262176 | tf_op jit(solution)/shard_map/ppermute | solution.py:330
  267.7 2.3 finish.1
  (144 shorter events, 69.0 us)
Async XLA Ops:
  3.0 13.0 %collective-permute-start.3 = (bf16[1,1536,256]{2,1,0:T(8,128)(2,1)S(1)}, bf16[1,1536,256]{2,1,0:T(8,128)(2,1)S(1)}, u32[]{:S(2)}, u32[]{:S(2)}) collective-permute-start(bf16[1,1536,256]{2,1,0:T(8,128)(2,1)S(1)} %get-tuple-element.76), channel_id=1, source_target_pairs={{0,8},{1,25},{8,0},{9,17},{16,24},{17,9},{24,16},{25,1},{32,40},{3... | collective-permute-start | bytes 2359304 | tf_op jit(solution)/shard_map/ppermute | solution.py:40
  6.6 13.1 %collective-permute-start = (bf16[1,1536,256]{2,1,0:T(8,128)(2,1)S(1)}, bf16[1,1536,256]{2,1,0:T(8,128)(2,1)S(1)}, u32[]{:S(2)}, u32[]{:S(2)}) collective-permute-start(bf16[1,1536,256]{2,1,0:T(8,128)(2,1)S(1)} %get-tuple-element.77), channel_id=1, source_target_pairs={{0,32},{1,97},{8,40},{9,105},{16,48},{17,113},{24,56},{25,121},{32... | collective-permute-start | bytes 2359304 | tf_op jit(solution)/shard_map/ppermute | solution.py:40
  17.3 19.9 %collective-permute-start.4 = (bf16[2,1536,256]{2,1,0:T(8,128)(2,1)}, bf16[2,1536,256]{2,1,0:T(8,128)(2,1)}, u32[]{:S(2)}, u32[]{:S(2)}) collective-permute-start(bf16[2,1536,256]{2,1,0:T(8,128)(2,1)} %pad_maximum_fusion.4), channel_id=1, source_target_pairs={{0,24},{1,9},{8,16},{9,1},{16,8},{17,25},{24,0},{25,17},{32,56},{3... | collective-permute-start | bytes 4718600 | tf_op jit(solution)/shard_map/ppermute | solution.py:40
  21.1 19.9 %collective-permute-start.1 = (bf16[2,1536,256]{2,1,0:T(8,128)(2,1)}, bf16[2,1536,256]{2,1,0:T(8,128)(2,1)}, u32[]{:S(2)}, u32[]{:S(2)}) collective-permute-start(bf16[2,1536,256]{2,1,0:T(8,128)(2,1)} %pad_maximum_fusion.3), channel_id=1, source_target_pairs={{0,96},{1,33},{8,104},{9,41},{16,112},{17,49},{24,120},{25,57},{32... | collective-permute-start | bytes 4718600 | tf_op jit(solution)/shard_map/ppermute | solution.py:40
  45.0 54.6 %collective-permute-start.2 = (bf16[4,1536,256]{2,1,0:T(8,128)(2,1)}, bf16[4,1536,256]{2,1,0:T(8,128)(2,1)}, u32[]{:S(2)}, u32[]{:S(2)}) collective-permute-start(bf16[4,1536,256]{2,1,0:T(8,128)(2,1)} %pad_maximum_fusion.refs_0_), channel_id=1, source_target_pairs={{0,8},{1,25},{8,0},{9,17},{16,24},{17,9},{24,16},{25,1},{32,40},{3... | collective-permute-start | bytes 9437192 | tf_op jit(solution)/shard_map/ppermute | solution.py:40
  47.2 57.6 %collective-permute-start.5 = (bf16[4,1536,256]{2,1,0:T(8,128)(2,1)}, bf16[4,1536,256]{2,1,0:T(8,128)(2,1)}, u32[]{:S(2)}, u32[]{:S(2)}) collective-permute-start(bf16[4,1536,256]{2,1,0:T(8,128)(2,1)} %pad_maximum_fusion.1.refs_2_.refs_1_), channel_id=1, source_target_pairs={{0,32},{1,97},{8,40},{9,105},{16,48},{17,113},{24,56},{25,121},{32... | collective-permute-start | bytes 9437192 | tf_op jit(solution)/shard_map/ppermute | solution.py:40
  61.2 58.6 %collective-permute-start.6 = (bf16[4,1536,256]{2,1,0:T(8,128)(2,1)}, bf16[4,1536,256]{2,1,0:T(8,128)(2,1)S(1)}, u32[]{:S(2)}, u32[]{:S(2)}) collective-permute-start(bf16[4,1536,256]{2,1,0:T(8,128)(2,1)} %pad_maximum_fusion.refs_0_), channel_id=1, source_target_pairs={{0,24},{1,9},{8,16},{9,1},{16,8},{17,25},{24,0},{25,17},{32,56},{3... | collective-permute-start | bytes 9437192 | tf_op jit(solution)/shard_map/ppermute | solution.py:40
  62.1 67.9 %collective-permute-start.7 = (bf16[4,1536,256]{2,1,0:T(8,128)(2,1)}, bf16[4,1536,256]{2,1,0:T(8,128)(2,1)S(1)}, u32[]{:S(2)}, u32[]{:S(2)}) collective-permute-start(bf16[4,1536,256]{2,1,0:T(8,128)(2,1)} %pad_maximum_fusion.1.refs_2_.refs_1_), channel_id=1, source_target_pairs={{0,96},{1,33},{8,104},{9,41},{16,112},{17,49},{24,120},{25,57},{32... | collective-permute-start | bytes 9437192 | tf_op jit(solution)/shard_map/ppermute | solution.py:40
  101.3 41.0 %collective-permute-start.8 = (bf16[4,1024,256]{2,1,0:T(8,128)(2,1)S(1)}, bf16[4,1024,256]{2,1,0:T(8,128)(2,1)S(1)}, u32[]{:S(2)}, u32[]{:S(2)}) collective-permute-start(bf16[4,1024,256]{2,1,0:T(8,128)(2,1)S(1)} %slice.148), channel_id=1, source_target_pairs={{0,24},{1,9},{8,16},{9,1},{16,8},{17,25},{24,0},{25,17},{32,56},{3... | collective-permute-start | bytes 6291464 | tf_op jit(solution)/shard_map/ppermute | solution.py:40
  106.5 37.8 %collective-permute-start.9 = (bf16[4,1024,256]{2,1,0:T(8,128)(2,1)S(1)}, bf16[4,1024,256]{2,1,0:T(8,128)(2,1)S(1)}, u32[]{:S(2)}, u32[]{:S(2)}) collective-permute-start(bf16[4,1024,256]{2,1,0:T(8,128)(2,1)S(1)} %slice.149), channel_id=1, source_target_pairs={{0,96},{1,33},{8,104},{9,41},{16,112},{17,49},{24,120},{25,57},{32... | collective-permute-start | bytes 6291464 | tf_op jit(solution)/shard_map/ppermute | solution.py:40
  109.0 54.6 %collective-permute-start.10 = (bf16[4,512,256]{2,1,0:T(8,128)(2,1)}, bf16[4,512,256]{2,1,0:T(8,128)(2,1)}, u32[]{:S(2)}, u32[]{:S(2)}) collective-permute-start(bf16[4,512,256]{2,1,0:T(8,128)(2,1)} %slice.150), channel_id=1, source_target_pairs={{0,24},{1,9},{8,16},{9,1},{16,8},{17,25},{24,0},{25,17},{32,56},{3... | collective-permute-start | bytes 3145736 | tf_op jit(solution)/shard_map/ppermute | solution.py:40
  119.7 43.8 %collective-permute-start.11 = (bf16[4,512,256]{2,1,0:T(8,128)(2,1)}, bf16[4,512,256]{2,1,0:T(8,128)(2,1)}, u32[]{:S(2)}, u32[]{:S(2)}) collective-permute-start(bf16[4,512,256]{2,1,0:T(8,128)(2,1)} %slice.151), channel_id=1, source_target_pairs={{0,96},{1,33},{8,104},{9,41},{16,112},{17,49},{24,120},{25,57},{32... | collective-permute-start | bytes 3145736 | tf_op jit(solution)/shard_map/ppermute | solution.py:40
  149.0 7.3 %collective-permute-start.12 = (bf16[4,128,128]{2,1,0:T(8,128)(2,1)S(1)}, bf16[4,128,128]{2,1,0:T(8,128)(2,1)S(1)}, u32[]{:S(2)}, u32[]{:S(2)}) collective-permute-start(bf16[4,128,128]{2,1,0:T(8,128)(2,1)S(1)} %convert_element_type.136), channel_id=1, source_target_pairs={{0,8},{8,0},{16,24},{24,16},{1,9},{9,1},{17,25},{25,17},{2,10},{10... | collective-permute-start | bytes 393224 | tf_op jit(solution)/shard_map/ppermute | solution.py:29
  150.7 8.6 %collective-permute-start.13 = (bf16[4,128,128]{2,1,0:T(8,128)(2,1)S(1)}, bf16[4,128,128]{2,1,0:T(8,128)(2,1)S(1)}, u32[]{:S(2)}, u32[]{:S(2)}) collective-permute-start(bf16[4,128,128]{2,1,0:T(8,128)(2,1)S(1)} %convert_element_type.136), channel_id=1, source_target_pairs={{0,24},{8,16},{16,8},{24,0},{1,25},{9,17},{17,9},{25,1},{2,26},{10... | collective-permute-start | bytes 393224 | tf_op jit(solution)/shard_map/ppermute | solution.py:29
  150.7 8.6 %collective-permute-start.14 = (bf16[4,128,128]{2,1,0:T(8,128)(2,1)S(1)}, bf16[4,128,128]{2,1,0:T(8,128)(2,1)S(1)}, u32[]{:S(2)}, u32[]{:S(2)}) collective-permute-start(bf16[4,128,128]{2,1,0:T(8,128)(2,1)S(1)} %convert_element_type.136), channel_id=1, source_target_pairs={{0,16},{8,24},{16,0},{24,8},{1,17},{9,25},{17,1},{25,9},{2,18},{10... | collective-permute-start | bytes 393224 | tf_op jit(solution)/shard_map/ppermute | solution.py:29
  160.0 8.7 %collective-permute-start.17 = (bf16[4,128,128]{2,1,0:T(8,128)(2,1)}, bf16[4,128,128]{2,1,0:T(8,128)(2,1)}, u32[]{:S(2)}, u32[]{:S(2)}) collective-permute-start(bf16[4,128,128]{2,1,0:T(8,128)(2,1)} %fusion.3), channel_id=1, source_target_pairs={{0,64},{32,96},{64,0},{96,32},{1,65},{33,97},{65,1},{97,33},{2,66}... | collective-permute-start | bytes 393224 | tf_op jit(solution)/shard_map/ppermute | solution.py:29
  162.3 8.1 %collective-permute-start.16 = (bf16[4,128,128]{2,1,0:T(8,128)(2,1)}, bf16[4,128,128]{2,1,0:T(8,128)(2,1)}, u32[]{:S(2)}, u32[]{:S(2)}) collective-permute-start(bf16[4,128,128]{2,1,0:T(8,128)(2,1)} %fusion.3), channel_id=1, source_target_pairs={{0,96},{32,64},{64,32},{96,0},{1,97},{33,65},{65,33},{97,1},{2,98}... | collective-permute-start | bytes 393224 | tf_op jit(solution)/shard_map/ppermute | solution.py:29
  163.0 7.4 %collective-permute-start.15 = (bf16[4,128,128]{2,1,0:T(8,128)(2,1)}, bf16[4,128,128]{2,1,0:T(8,128)(2,1)}, u32[]{:S(2)}, u32[]{:S(2)}) collective-permute-start(bf16[4,128,128]{2,1,0:T(8,128)(2,1)} %fusion.3), channel_id=1, source_target_pairs={{0,32},{32,0},{64,96},{96,64},{1,33},{33,1},{65,97},{97,65},{2,34}... | collective-permute-start | bytes 393224 | tf_op jit(solution)/shard_map/ppermute | solution.py:29
  175.0 9.4 %collective-permute-start.18 = (bf16[4,128,128]{2,1,0:T(8,128)(2,1)S(1)}, bf16[4,128,128]{2,1,0:T(8,128)(2,1)S(1)}, u32[]{:S(2)}, u32[]{:S(2)}) collective-permute-start(bf16[4,128,128]{2,1,0:T(8,128)(2,1)S(1)} %convert_element_type.144), channel_id=1, source_target_pairs={{0,8},{8,0},{16,24},{24,16},{1,9},{9,1},{17,25},{25,17},{2,10},{10... | collective-permute-start | bytes 393224 | tf_op jit(solution)/shard_map/ppermute | solution.py:29
  175.1 9.3 %collective-permute-start.19 = (bf16[4,128,128]{2,1,0:T(8,128)(2,1)S(1)}, bf16[4,128,128]{2,1,0:T(8,128)(2,1)S(1)}, u32[]{:S(2)}, u32[]{:S(2)}) collective-permute-start(bf16[4,128,128]{2,1,0:T(8,128)(2,1)S(1)} %convert_element_type.144), channel_id=1, source_target_pairs={{0,24},{8,16},{16,8},{24,0},{1,25},{9,17},{17,9},{25,1},{2,26},{10... | collective-permute-start | bytes 393224 | tf_op jit(solution)/shard_map/ppermute | solution.py:29
  177.0 7.3 %collective-permute-start.20 = (bf16[4,128,128]{2,1,0:T(8,128)(2,1)S(1)}, bf16[4,128,128]{2,1,0:T(8,128)(2,1)S(1)}, u32[]{:S(2)}, u32[]{:S(2)}) collective-permute-start(bf16[4,128,128]{2,1,0:T(8,128)(2,1)S(1)} %convert_element_type.144), channel_id=1, source_target_pairs={{0,16},{8,24},{16,0},{24,8},{1,17},{9,25},{17,1},{25,9},{2,18},{10... | collective-permute-start | bytes 393224 | tf_op jit(solution)/shard_map/ppermute | solution.py:29
  187.1 7.2 %collective-permute-start.22 = (bf16[4,128,128]{2,1,0:T(8,128)(2,1)S(1)}, bf16[4,128,128]{2,1,0:T(8,128)(2,1)S(1)}, u32[]{:S(2)}, u32[]{:S(2)}) collective-permute-start(bf16[4,128,128]{2,1,0:T(8,128)(2,1)S(1)} %convert_add_fusion.4), channel_id=1, source_target_pairs={{0,96},{32,64},{64,32},{96,0},{1,97},{33,65},{65,33},{97,1},{2,98}... | collective-permute-start | bytes 393224 | tf_op jit(solution)/shard_map/ppermute | solution.py:29
  187.8 6.5 %collective-permute-start.21 = (bf16[4,128,128]{2,1,0:T(8,128)(2,1)S(1)}, bf16[4,128,128]{2,1,0:T(8,128)(2,1)S(1)}, u32[]{:S(2)}, u32[]{:S(2)}) collective-permute-start(bf16[4,128,128]{2,1,0:T(8,128)(2,1)S(1)} %convert_add_fusion.4), channel_id=1, source_target_pairs={{0,32},{32,0},{64,96},{96,64},{1,33},{33,1},{65,97},{97,65},{2,34}... | collective-permute-start | bytes 393224 | tf_op jit(solution)/shard_map/ppermute | solution.py:29
  207.4 9.3 %collective-permute-start.24 = (bf16[256,2048]{1,0:T(8,128)(2,1)}, bf16[256,2048]{1,0:T(8,128)(2,1)}, u32[]{:S(2)}, u32[]{:S(2)}) collective-permute-start(bf16[256,2048]{1,0:T(8,128)(2,1)} %get-tuple-element.59), channel_id=1, source_target_pairs={{0,1},{1,0},{2,3},{3,2},{4,5},{5,4},{6,7},{7,6},{8,9},{9,8},{10,11... | collective-permute-start | bytes 3145736 | tf_op jit(solution)/shard_map/ppermute | solution.py:29
  216.4 12.3 %collective-permute-start.28 = (bf16[256,2048]{1,0:T(8,128)(2,1)}, bf16[256,2048]{1,0:T(8,128)(2,1)S(1)}, u32[]{:S(2)}, u32[]{:S(2)}) collective-permute-start(bf16[256,2048]{1,0:T(8,128)(2,1)} %get-tuple-element.65), channel_id=1, source_target_pairs={{0,1},{1,0},{2,3},{3,2},{4,5},{5,4},{6,7},{7,6},{8,9},{9,8},{10,11... | collective-permute-start | bytes 3145736 | tf_op jit(solution)/shard_map/ppermute | solution.py:29
  217.8 12.4 %collective-permute-start.25 = (bf16[128,2048]{1,0:T(8,128)(2,1)S(1)}, bf16[128,2048]{1,0:T(8,128)(2,1)S(1)}, u32[]{:S(2)}, u32[]{:S(2)}) collective-permute-start(bf16[128,2048]{1,0:T(8,128)(2,1)S(1)} %add_convert_fusion.3), channel_id=1, source_target_pairs={{0,2},{1,7},{2,0},{3,5},{4,6},{5,3},{6,4},{7,1},{8,10},{9,15},{10,... | collective-permute-start | bytes 1572872 | tf_op jit(solution)/shard_map/ppermute | solution.py:330
  228.4 12.0 %collective-permute-start.27 = (bf16[256,2048]{1,0:T(8,128)(2,1)}, bf16[256,2048]{1,0:T(8,128)(2,1)S(1)}, u32[]{:S(2)}, u32[]{:S(2)}) collective-permute-start(bf16[256,2048]{1,0:T(8,128)(2,1)} %get-tuple-element.63), channel_id=1, source_target_pairs={{0,1},{1,0},{2,3},{3,2},{4,5},{5,4},{6,7},{7,6},{8,9},{9,8},{10,11... | collective-permute-start | bytes 3145736 | tf_op jit(solution)/shard_map/ppermute | solution.py:29
  228.9 12.5 %collective-permute-start.30 = (bf16[128,2048]{1,0:T(8,128)(2,1)S(1)}, bf16[128,2048]{1,0:T(8,128)(2,1)S(1)}, u32[]{:S(2)}, u32[]{:S(2)}) collective-permute-start(bf16[128,2048]{1,0:T(8,128)(2,1)S(1)} %add_convert_fusion.1), channel_id=1, source_target_pairs={{0,2},{1,7},{2,0},{3,5},{4,6},{5,3},{6,4},{7,1},{8,10},{9,15},{10,... | collective-permute-start | bytes 1572872 | tf_op jit(solution)/shard_map/ppermute | solution.py:330
  240.5 14.9 %collective-permute-start.32 = (bf16[128,2048]{1,0:T(8,128)(2,1)S(1)}, bf16[128,2048]{1,0:T(8,128)(2,1)S(1)}, u32[]{:S(2)}, u32[]{:S(2)}) collective-permute-start(bf16[128,2048]{1,0:T(8,128)(2,1)S(1)} %add_convert_fusion.2), channel_id=1, source_target_pairs={{0,2},{1,7},{2,0},{3,5},{4,6},{5,3},{6,4},{7,1},{8,10},{9,15},{10,... | collective-permute-start | bytes 1572872 | tf_op jit(solution)/shard_map/ppermute | solution.py:330
  241.7 14.0 %collective-permute-start.31 = (bf16[64,2048]{1,0:T(8,128)(2,1)S(1)}, bf16[64,2048]{1,0:T(8,128)(2,1)S(1)}, u32[]{:S(2)}, u32[]{:S(2)}) collective-permute-start(bf16[64,2048]{1,0:T(8,128)(2,1)S(1)} %slice.198), channel_id=1, source_target_pairs={{0,6},{1,3},{2,4},{3,1},{4,2},{5,7},{6,0},{7,5},{8,14},{9,11},{10,... | collective-permute-start | bytes 786440 | tf_op jit(solution)/shard_map/ppermute | solution.py:330
  242.5 19.5 %collective-permute-start.34 = (bf16[128,2048]{1,0:T(8,128)(2,1)S(1)}, bf16[128,2048]{1,0:T(8,128)(2,1)S(1)}, u32[]{:S(2)}, u32[]{:S(2)}) collective-permute-start(bf16[128,2048]{1,0:T(8,128)(2,1)S(1)} %add_convert_fusion), channel_id=1, source_target_pairs={{0,2},{1,7},{2,0},{3,5},{4,6},{5,3},{6,4},{7,1},{8,10},{9,15},{10,... | collective-permute-start | bytes 1572872 | tf_op jit(solution)/shard_map/ppermute | solution.py:330
  255.7 7.3 %collective-permute-start.33 = (bf16[64,2048]{1,0:T(8,128)(2,1)S(1)}, bf16[64,2048]{1,0:T(8,128)(2,1)S(1)}, u32[]{:S(2)}, u32[]{:S(2)}) collective-permute-start(bf16[64,2048]{1,0:T(8,128)(2,1)S(1)} %slice.197), channel_id=1, source_target_pairs={{0,6},{1,3},{2,4},{3,1},{4,2},{5,7},{6,0},{7,5},{8,14},{9,11},{10,... | collective-permute-start | bytes 786440 | tf_op jit(solution)/shard_map/ppermute | solution.py:330
  (28 other events, 179.7 us)

commit v2 on v1

--- a/solution.py
+++ b/solution.py
@@ -418,7 +418,7 @@
             pltpu.SemaphoreType.DMA,
         ],
         cost_estimate=pl.CostEstimate(flops=2 * n * 1536 * 2048, bytes_accessed=1536 * 4096, transcendentals=0),
-        compiler_params=pltpu.CompilerParams(vmem_limit_bytes=30 << 20),
+        compiler_params=pltpu.CompilerParams(vmem_limit_bytes=54 << 20),
         name="collect",
     )(row_table(), pre_kv, grad_k, grad_v, back_q, later, *weights)
 

time: 276 us -> 270 us (0.978)
  local copies, waits for them, and re-layouts: 28.8 us -> 23 us
    unnamed x48 -> x38, local copies, waits for them, and re-layouts: 17.2 us -> 10.9 us
  transfers between devices with their start and end apart: 36 -> 36, of which waited for: 18 -> 18; matrix products, arithmetic and copies ran while one was open for 7% -> 6% of each run, Pallas kernels for 20% -> 20%
where the time goes in v2:
time: 270 us; the launch traced here: 265 us
  waiting for transfers between devices  122 us (45%)
  Pallas kernels  68.2 us (25%)
  starting transfers between devices  37.7 us (14%)
  local copies, waits for them, and re-layouts  23 us (9%)
  other arithmetic  13 us (5%)
    ppermute x12, waiting for transfers between devices, swap_links(): return lax.ppermute(x, ('z', 'y', 'c'), pairs)  85.1 us
    pallas_call x3, Pallas kernels, push(): pl.pallas_call(functools.partial(push_kernel, kinds, counts), in_specs=[h...  23.4 us
    ppermute x8, waiting for transfers between devices, swap_rings(): return lax.ppermute(a, ('x', 'c'), pairs)  22.4 us
    pallas_call x4, Pallas kernels, project(): pl.pallas_call(functools.partial(project_kernel, slots, len(start), heads...  20.3 us
    ppermute x16, starting transfers between devices, swap(): return lax.ppermute(x, axis, [(i, i ^ offset) for i in range(n)])  15 us
    ppermute x16, waiting for transfers between devices, swap(): return lax.ppermute(x, axis, [(i, i ^ offset) for i in range(n)])  14.3 us
    ppermute x12, starting transfers between devices, swap_links(): return lax.ppermute(x, ('z', 'y', 'c'), pairs)  14 us
    unnamed x38, local copies, waits for them, and re-layouts  10.9 us
  transfers between devices with their start and end apart: 36, of which 18 were waited for; matrix products, arithmetic and copies ran while one was open for 6% of the time, Pallas kernels for 20%

profile of v2, /device:TPU:1, one launch (start us, length us, event | category | flops | bytes accessed | tf_op | source)
XLA Modules:
  0.0 264.8 jit_solution(12453979586393340183)
XLA Ops:
  3.0 3.6 %collective-permute-start.3 = (bf16[1,1536,256]{2,1,0:T(8,128)(2,1)S(1)}, bf16[1,1536,256]{2,1,0:T(8,128)(2,1)S(1)}, u32[]{:S(2)}, u32[]{:S(2)}) collective-permute-start(bf16[1,1536,256]{2,1,0:T(8,128)(2,1)S(1)} %get-tuple-element.76), channel_id=1, source_target_pairs={{0,8},{1,25},{8,0},{9,17},{16,24},{17,9},{24,16},{25,1},{32,40},{3... | collective-permute-start | bytes 2359304 | tf_op jit(solution)/shard_map/ppermute | solution.py:40
  6.6 3.8 %collective-permute-start = (bf16[1,1536,256]{2,1,0:T(8,128)(2,1)S(1)}, bf16[1,1536,256]{2,1,0:T(8,128)(2,1)S(1)}, u32[]{:S(2)}, u32[]{:S(2)}) collective-permute-start(bf16[1,1536,256]{2,1,0:T(8,128)(2,1)S(1)} %get-tuple-element.77), channel_id=1, source_target_pairs={{0,32},{1,97},{8,40},{9,105},{16,48},{17,113},{24,56},{25,121},{32... | collective-permute-start | bytes 2359304 | tf_op jit(solution)/shard_map/ppermute | solution.py:40
  10.4 5.6 %collective-permute-done.3 = bf16[1,1536,256]{2,1,0:T(8,128)(2,1)S(1)} collective-permute-done((bf16[1,1536,256]{2,1,0:T(8,128)(2,1)S(1)}, bf16[1,1536,256]{2,1,0:T(8,128)(2,1)S(1)}, u32[]{:S(2)}, u32[]{:S(2)}) %collective-permute-start.3) | collective-permute-done | bytes 786464 | tf_op jit(solution)/shard_map/ppermute | solution.py:40
  21.1 16.1 %collective-permute-done.4 = bf16[2,1536,256]{2,1,0:T(8,128)(2,1)} collective-permute-done((bf16[2,1536,256]{2,1,0:T(8,128)(2,1)}, bf16[2,1536,256]{2,1,0:T(8,128)(2,1)}, u32[]{:S(2)}, u32[]{:S(2)}) %collective-permute-start.4) | collective-permute-done | bytes 1572896 | tf_op jit(solution)/shard_map/ppermute | solution.py:40
  37.2 3.8 %collective-permute-done.1 = bf16[2,1536,256]{2,1,0:T(8,128)(2,1)} collective-permute-done((bf16[2,1536,256]{2,1,0:T(8,128)(2,1)}, bf16[2,1536,256]{2,1,0:T(8,128)(2,1)}, u32[]{:S(2)}, u32[]{:S(2)}) %collective-permute-start.1) | collective-permute-done | bytes 1572896 | tf_op jit(solution)/shard_map/ppermute | solution.py:40
  47.3 3.6 %collective-permute-start.5 = (bf16[4,1536,256]{2,1,0:T(8,128)(2,1)}, bf16[4,1536,256]{2,1,0:T(8,128)(2,1)}, u32[]{:S(2)}, u32[]{:S(2)}) collective-permute-start(bf16[4,1536,256]{2,1,0:T(8,128)(2,1)} %pad_maximum_fusion.1.refs_2_.refs_1_), channel_id=1, source_target_pairs={{0,32},{1,97},{8,40},{9,105},{16,48},{17,113},{24,56},{25,121},{32... | collective-permute-start | bytes 9437192 | tf_op jit(solution)/shard_map/ppermute | solution.py:40
  51.3 3.4 %copy-done.1 = bf16[512,8192]{1,0:T(8,128)(2,1)S(1)} copy-done((bf16[512,8192]{1,0:T(8,128)(2,1)S(1)}, bf16[512,8192]{1,0:T(8,128)(2,1)}, u32[]{:S(2)}) %copy-start.1) | copy-done | bytes 8388632
  54.7 6.5 %reorder_columns.1 = (bf16[8,256,512]{2,1,0:T(8,128)(2,1)S(1)}, bf16[4,256,512]{2,1,0:T(8,128)(2,1)S(1)}, bf16[4,256,512]{2,1,0:T(8,128)(2,1)S(1)}, bf16[8,256,5...) custom-call(s32[2,16]{1,0:T(2,128)S(1)} %pad_add_fusion.table, ...), custom_call_target="tpu_custom_call" | custom-call | bytes 16777216 | tf_op jit(solution)/shard_map/reorder_columns/pallas_call | solution.py:107
  62.2 37.5 %collective-permute-done.2.refs_1_ = bf16[4,1536,256]{2,1,0:T(8,128)(2,1)} collective-permute-done((bf16[4,1536,256]{2,1,0:T(8,128)(2,1)}, bf16[4,1536,256]{2,1,0:T(8,128)(2,1)}, u32[]{:S(2)}, u32[]{:S(2)}) %collective-permute-start.2) | collective-permute-done | bytes 3145760 | tf_op jit(solution)/shard_map/ppermute | solution.py:40
  101.5 3.3 %collective-permute-done.5.refs_3_.refs_1_ = bf16[4,1536,256]{2,1,0:T(8,128)(2,1)} collective-permute-done((bf16[4,1536,256]{2,1,0:T(8,128)(2,1)}, bf16[4,1536,256]{2,1,0:T(8,128)(2,1)}, u32[]{:S(2)}, u32[]{:S(2)}) %collective-permute-start.5) | collective-permute-done | bytes 3145760 | tf_op jit(solution)/shard_map/ppermute | solution.py:40
  106.7 2.3 slice.150
  112.3 7.5 %collective-permute-done.6.refs_2_ = bf16[4,1536,256]{2,1,0:T(8,128)(2,1)S(1)} collective-permute-done((bf16[4,1536,256]{2,1,0:T(8,128)(2,1)}, bf16[4,1536,256]{2,1,0:T(8,128)(2,1)S(1)}, u32[]{:S(2)}, u32[]{:S(2)}) %collective-permute-start.6) | collective-permute-done | bytes 3145760 | tf_op jit(solution)/shard_map/ppermute | solution.py:40
  120.0 10.1 %project.4 = (f32[1024,512]{1,0:T(8,128)S(1)}, f32[512,512]{1,0:T(8,128)S(1)}) custom-call(bf16[4,1536,256]{2,1,0:T(8,128)(2,1)} %pad_maximum_fusion.refs_0_, bf16[4,1536,256]{2,1,0:T(8,128)(2,1)} %collective-permute-done.2.refs_1_, bf16[4,1536,256]{2,1,0:T(8,128)(2,1)} %pad_maximum_fusion.1.refs_2_.refs_1_, ...), custom_call_target="tpu_custom_call" | custom-call | flops 6442450944 | bytes 12582912 | tf_op jit(solution)/shard_map/project/pallas_call | solution.py:218
  130.1 4.2 %project.5 = (f32[1024,512]{1,0:T(8,128)S(1)}, f32[512,512]{1,0:T(8,128)S(1)}) custom-call(f32[1024,512]{1,0:T(8,128)S(1)} %get-tuple-element.40.refs_0_, f32[512,512]{1,0:T(8,128)S(1)} %get-tuple-element.41.refs_1_, bf16[4,1536,256]{2,1,0:T(8,128)(2,1)S(1)} %collective-permute-done.6.refs_2_, ...), custom_call_target="tpu_custom_call" | custom-call | flops 3221225472 | bytes 6291456 | tf_op jit(solution)/shard_map/project/pallas_call | solution.py:218
  135.3 7.1 %collective-permute-done.8.refs_1_ = bf16[4,1024,256]{2,1,0:T(8,128)(2,1)S(1)} collective-permute-done((bf16[4,1024,256]{2,1,0:T(8,128)(2,1)S(1)}, bf16[4,1024,256]{2,1,0:T(8,128)(2,1)S(1)}, u32[]{:S(2)}, u32[]{:S(2)}) %collective-permute-start.8) | collective-permute-done | bytes 2097184 | tf_op jit(solution)/shard_map/ppermute | solution.py:40
  145.7 3.3 %project.6 = (f32[1024,512]{1,0:T(8,128)S(1)}, f32[4,128,128]{2,1,0:T(8,128)S(1)}) custom-call(f32[1024,512]{1,0:T(8,128)S(1)} %get-tuple-element.48.refs_0_, bf16[4,1024,256]{2,1,0:T(8,128)(2,1)S(1)} %collective-permute-done.8.refs_1_, bf16[4,1024,256]{2,1,0:T(8,128)(2,1)} %copy-done.13, bf16[4,256,512]{2,1,0:T(8,128)(2,1)S(1)} %get-tuple-element.43.refs_3_, ...), custom_call_target="tpu_custom_call" | custom-call | flops 2147483648 | bytes 4194304 | tf_op jit(solution)/shard_map/project/pallas_call | solution.py:218
  152.6 3.7 %collective-permute-done.12 = bf16[4,128,128]{2,1,0:T(8,128)(2,1)S(1)} collective-permute-done((bf16[4,128,128]{2,1,0:T(8,128)(2,1)S(1)}, bf16[4,128,128]{2,1,0:T(8,128)(2,1)S(1)}, u32[]{:S(2)}, u32[]{:S(2)}) %collective-permute-start.12) | collective-permute-done | bytes 131104 | tf_op jit(solution)/shard_map/ppermute | solution.py:29
  156.3 3.0 %collective-permute-done.13 = bf16[4,128,128]{2,1,0:T(8,128)(2,1)S(1)} collective-permute-done((bf16[4,128,128]{2,1,0:T(8,128)(2,1)S(1)}, bf16[4,128,128]{2,1,0:T(8,128)(2,1)S(1)}, u32[]{:S(2)}, u32[]{:S(2)}) %collective-permute-start.13) | collective-permute-done | bytes 131104 | tf_op jit(solution)/shard_map/ppermute | solution.py:29
  160.1 2.3 collective-permute-start.17
  166.1 2.7 %project.7.pre_q = f32[512,512]{1,0:T(8,128)S(1)} custom-call(f32[512,512]{1,0:T(8,128)S(1)} %copy-done.6, bf16[4,512,256]{2,1,0:T(8,128)(2,1)} %collective-permute-done.10.refs_1_.refs_2_, bf16[4,512,256]{2,1,0:T(8,128)(2,1)} %collective-permute-done.11.refs_2_.refs_3_, bf16[4,256,512]{2,1,0:T(8,128)(2,1)S(1)} %get-tuple-element.43.refs_3_, ...), custom_call_target="tpu_custom_call" | custom-call | flops 1073741824 | bytes 2097152 | tf_op jit(solution)/shard_map/project/pallas_call | solution.py:218
  171.7 3.3 %attend.1 = (f32[4,128,128]{2,1,0:T(8,128)S(1)}, bf16[512,512]{1,0:T(8,128)(2,1)S(1)}) custom-call(f32[512,512]{1,0:T(8,128)S(1)} %project.7.pre_q, f32[1024,512]{1,0:T(8,128)S(1)} %get-tuple-element.49.pre_k.pre_v.pre_kv, f32[1024,512]{1,0:T(8,128)S(1)} %get-tuple-element.49.pre_k.pre_v.pre_kv, f32[4,128,128]{2,1,0:T(8,128)S(1)} %fusion.2.before, ...), custom_call_target="tpu_custom_call" | custom-call | tf_op jit(solution)/shard_map/attend/pallas_call | solution.py:281
  178.5 3.8 %attend_back.1 = (bf16[512,512]{1,0:T(8,128)(2,1)S(1)}, f32[512,512]{1,0:T(8,128)S(1)}, f32[512,512]{1,0:T(8,128)S(1)}) custom-call(f32[512,512]{1,0:T(8,128)S(1)} %project.7.pre_q, f32[1024,512]{1,0:T(8,128)S(1)} %get-tuple-element.49.pre_k.pre_v.pre_kv, f32[1024,512]{1,0:T(8,128)S(1)} %get-tuple-element.49.pre_k.pre_v.pre_kv, ...), custom_call_target="tpu_custom_call" | custom-call | flops 805306368 | bytes 4194304 | tf_op jit(solution)/shard_map/attend_back/pallas_call | solution.py:299
  190.4 3.8 %collective-permute-done.22 = bf16[4,128,128]{2,1,0:T(8,128)(2,1)S(1)} collective-permute-done((bf16[4,128,128]{2,1,0:T(8,128)(2,1)S(1)}, bf16[4,128,128]{2,1,0:T(8,128)(2,1)S(1)}, u32[]{:S(2)}, u32[]{:S(2)}) %collective-permute-start.22) | collective-permute-done | bytes 131104 | tf_op jit(solution)/shard_map/ppermute | solution.py:29
  195.1 8.6 %collect.1 = (bf16[512,1536]{1,0:T(8,128)(2,1)}, bf16[256,2048]{1,0:T(8,128)(2,1)}, bf16[256,2048]{1,0:T(8,128)(2,1)}) custom-call(s32[8]{0:T(128)} %stack.308.table, f32[1024,512]{1,0:T(8,128)} %copy-done, f32[512,512]{1,0:T(8,128)} %copy-done.10, f32[512,512]{1,0:T(8,128)} %copy-done.11, bf16[512,512]{1,0:T(8,128)(2,1)} %copy-done.12, ...), custom_call_target="tpu_custom_call" | custom-call | flops 3221225472 | bytes 6291456 | tf_op jit(solution)/shard_map/collect/pallas_call | solution.py:408
  205.1 7.8 %push.4 = (bf16[256,2048]{1,0:T(8,128)(2,1)}, bf16[256,2048]{1,0:T(8,128)(2,1)}) custom-call(bf16[512,1536]{1,0:T(8,128)(2,1)} %get-tuple-element.66.refs_0_, bf16[4,1536,256]{2,1,0:T(8,128)(2,1)} %collective-permute-done.2.refs_1_, bf16[4,1536,256]{2,1,0:T(8,128)(2,1)} %copy-done.9), custom_call_target="tpu_custom_call" | custom-call | flops 3221225472 | bytes 1 | tf_op jit(solution)/shard_map/push/pallas_call | solution.py:459
  213.3 2.6 collective-permute-start.25
  215.8 8.0 %push.3 = (bf16[256,2048]{1,0:T(8,128)(2,1)}, bf16[256,2048]{1,0:T(8,128)(2,1)}) custom-call(bf16[512,1536]{1,0:T(8,128)(2,1)} %get-tuple-element.66.refs_0_, bf16[4,1536,256]{2,1,0:T(8,128)(2,1)} %pad_maximum_fusion.1.refs_2_.refs_1_, bf16[4,1024,256]{2,1,0:T(8,128)(2,1)} %copy-done.13, bf16[4,512,256]{2,1,0:T(8,128)(2,1)} %collective-permute-done.11.refs_2_.refs_3_), custom_call_target="tpu_custom_call" | custom-call | flops 3221225472 | bytes 1 | tf_op jit(solution)/shard_map/push/pallas_call | solution.py:459
  225.7 7.7 %push.5 = (bf16[256,2048]{1,0:T(8,128)(2,1)}, bf16[256,2048]{1,0:T(8,128)(2,1)}) custom-call(bf16[512,1536]{1,0:T(8,128)(2,1)} %get-tuple-element.66.refs_0_, bf16[4,1536,256]{2,1,0:T(8,128)(2,1)} %collective-permute-done.5.refs_3_.refs_1_, bf16[4,1536,256]{2,1,0:T(8,128)(2,1)} %copy-done.8), custom_call_target="tpu_custom_call" | custom-call | flops 3221225472 | bytes 1 | tf_op jit(solution)/shard_map/push/pallas_call | solution.py:459
  239.3 10.4 %collective-permute-done.32 = bf16[128,2048]{1,0:T(8,128)(2,1)S(1)} collective-permute-done((bf16[128,2048]{1,0:T(8,128)(2,1)S(1)}, bf16[128,2048]{1,0:T(8,128)(2,1)S(1)}, u32[]{:S(2)}, u32[]{:S(2)}) %collective-permute-start.32) | collective-permute-done | bytes 524320 | tf_op jit(solution)/shard_map/ppermute | solution.py:330
  250.1 6.2 %collective-permute-done.34 = bf16[128,2048]{1,0:T(8,128)(2,1)S(1)} collective-permute-done((bf16[128,2048]{1,0:T(8,128)(2,1)S(1)}, bf16[128,2048]{1,0:T(8,128)(2,1)S(1)}, u32[]{:S(2)}, u32[]{:S(2)}) %collective-permute-start.34) | collective-permute-done | bytes 524320 | tf_op jit(solution)/shard_map/ppermute | solution.py:330
  257.2 4.7 %collective-permute-done.35 = bf16[64,2048]{1,0:T(8,128)(2,1)S(1)} collective-permute-done((bf16[64,2048]{1,0:T(8,128)(2,1)S(1)}, bf16[64,2048]{1,0:T(8,128)(2,1)S(1)}, u32[]{:S(2)}, u32[]{:S(2)}) %collective-permute-start.35) | collective-permute-done | bytes 262176 | tf_op jit(solution)/shard_map/ppermute | solution.py:330
  262.0 2.3 finish.1
  (134 shorter events, 61.2 us)
Async XLA Ops:
  3.0 13.0 %collective-permute-start.3 = (bf16[1,1536,256]{2,1,0:T(8,128)(2,1)S(1)}, bf16[1,1536,256]{2,1,0:T(8,128)(2,1)S(1)}, u32[]{:S(2)}, u32[]{:S(2)}) collective-permute-start(bf16[1,1536,256]{2,1,0:T(8,128)(2,1)S(1)} %get-tuple-element.76), channel_id=1, source_target_pairs={{0,8},{1,25},{8,0},{9,17},{16,24},{17,9},{24,16},{25,1},{32,40},{3... | collective-permute-start | bytes 2359304 | tf_op jit(solution)/shard_map/ppermute | solution.py:40
  6.6 13.1 %collective-permute-start = (bf16[1,1536,256]{2,1,0:T(8,128)(2,1)S(1)}, bf16[1,1536,256]{2,1,0:T(8,128)(2,1)S(1)}, u32[]{:S(2)}, u32[]{:S(2)}) collective-permute-start(bf16[1,1536,256]{2,1,0:T(8,128)(2,1)S(1)} %get-tuple-element.77), channel_id=1, source_target_pairs={{0,32},{1,97},{8,40},{9,105},{16,48},{17,113},{24,56},{25,121},{32... | collective-permute-start | bytes 2359304 | tf_op jit(solution)/shard_map/ppermute | solution.py:40
  17.3 19.9 %collective-permute-start.4 = (bf16[2,1536,256]{2,1,0:T(8,128)(2,1)}, bf16[2,1536,256]{2,1,0:T(8,128)(2,1)}, u32[]{:S(2)}, u32[]{:S(2)}) collective-permute-start(bf16[2,1536,256]{2,1,0:T(8,128)(2,1)} %pad_maximum_fusion.4), channel_id=1, source_target_pairs={{0,24},{1,9},{8,16},{9,1},{16,8},{17,25},{24,0},{25,17},{32,56},{3... | collective-permute-start | bytes 4718600 | tf_op jit(solution)/shard_map/ppermute | solution.py:40
  21.1 19.9 %collective-permute-start.1 = (bf16[2,1536,256]{2,1,0:T(8,128)(2,1)}, bf16[2,1536,256]{2,1,0:T(8,128)(2,1)}, u32[]{:S(2)}, u32[]{:S(2)}) collective-permute-start(bf16[2,1536,256]{2,1,0:T(8,128)(2,1)} %pad_maximum_fusion.3), channel_id=1, source_target_pairs={{0,96},{1,33},{8,104},{9,41},{16,112},{17,49},{24,120},{25,57},{32... | collective-permute-start | bytes 4718600 | tf_op jit(solution)/shard_map/ppermute | solution.py:40
  45.1 54.6 %collective-permute-start.2 = (bf16[4,1536,256]{2,1,0:T(8,128)(2,1)}, bf16[4,1536,256]{2,1,0:T(8,128)(2,1)}, u32[]{:S(2)}, u32[]{:S(2)}) collective-permute-start(bf16[4,1536,256]{2,1,0:T(8,128)(2,1)} %pad_maximum_fusion.refs_0_), channel_id=1, source_target_pairs={{0,8},{1,25},{8,0},{9,17},{16,24},{17,9},{24,16},{25,1},{32,40},{3... | collective-permute-start | bytes 9437192 | tf_op jit(solution)/shard_map/ppermute | solution.py:40
  47.3 57.6 %collective-permute-start.5 = (bf16[4,1536,256]{2,1,0:T(8,128)(2,1)}, bf16[4,1536,256]{2,1,0:T(8,128)(2,1)}, u32[]{:S(2)}, u32[]{:S(2)}) collective-permute-start(bf16[4,1536,256]{2,1,0:T(8,128)(2,1)} %pad_maximum_fusion.1.refs_2_.refs_1_), channel_id=1, source_target_pairs={{0,32},{1,97},{8,40},{9,105},{16,48},{17,113},{24,56},{25,121},{32... | collective-permute-start | bytes 9437192 | tf_op jit(solution)/shard_map/ppermute | solution.py:40
  61.2 58.6 %collective-permute-start.6 = (bf16[4,1536,256]{2,1,0:T(8,128)(2,1)}, bf16[4,1536,256]{2,1,0:T(8,128)(2,1)S(1)}, u32[]{:S(2)}, u32[]{:S(2)}) collective-permute-start(bf16[4,1536,256]{2,1,0:T(8,128)(2,1)} %pad_maximum_fusion.refs_0_), channel_id=1, source_target_pairs={{0,24},{1,9},{8,16},{9,1},{16,8},{17,25},{24,0},{25,17},{32,56},{3... | collective-permute-start | bytes 9437192 | tf_op jit(solution)/shard_map/ppermute | solution.py:40
  62.2 67.9 %collective-permute-start.7 = (bf16[4,1536,256]{2,1,0:T(8,128)(2,1)}, bf16[4,1536,256]{2,1,0:T(8,128)(2,1)S(1)}, u32[]{:S(2)}, u32[]{:S(2)}) collective-permute-start(bf16[4,1536,256]{2,1,0:T(8,128)(2,1)} %pad_maximum_fusion.1.refs_2_.refs_1_), channel_id=1, source_target_pairs={{0,96},{1,33},{8,104},{9,41},{16,112},{17,49},{24,120},{25,57},{32... | collective-permute-start | bytes 9437192 | tf_op jit(solution)/shard_map/ppermute | solution.py:40
  101.4 41.0 %collective-permute-start.8 = (bf16[4,1024,256]{2,1,0:T(8,128)(2,1)S(1)}, bf16[4,1024,256]{2,1,0:T(8,128)(2,1)S(1)}, u32[]{:S(2)}, u32[]{:S(2)}) collective-permute-start(bf16[4,1024,256]{2,1,0:T(8,128)(2,1)S(1)} %slice.148), channel_id=1, source_target_pairs={{0,24},{1,9},{8,16},{9,1},{16,8},{17,25},{24,0},{25,17},{32,56},{3... | collective-permute-start | bytes 6291464 | tf_op jit(solution)/shard_map/ppermute | solution.py:40
  106.6 37.8 %collective-permute-start.9 = (bf16[4,1024,256]{2,1,0:T(8,128)(2,1)S(1)}, bf16[4,1024,256]{2,1,0:T(8,128)(2,1)S(1)}, u32[]{:S(2)}, u32[]{:S(2)}) collective-permute-start(bf16[4,1024,256]{2,1,0:T(8,128)(2,1)S(1)} %slice.149), channel_id=1, source_target_pairs={{0,96},{1,33},{8,104},{9,41},{16,112},{17,49},{24,120},{25,57},{32... | collective-permute-start | bytes 6291464 | tf_op jit(solution)/shard_map/ppermute | solution.py:40
  109.0 54.6 %collective-permute-start.10 = (bf16[4,512,256]{2,1,0:T(8,128)(2,1)}, bf16[4,512,256]{2,1,0:T(8,128)(2,1)}, u32[]{:S(2)}, u32[]{:S(2)}) collective-permute-start(bf16[4,512,256]{2,1,0:T(8,128)(2,1)} %slice.150), channel_id=1, source_target_pairs={{0,24},{1,9},{8,16},{9,1},{16,8},{17,25},{24,0},{25,17},{32,56},{3... | collective-permute-start | bytes 3145736 | tf_op jit(solution)/shard_map/ppermute | solution.py:40
  119.8 43.8 %collective-permute-start.11 = (bf16[4,512,256]{2,1,0:T(8,128)(2,1)}, bf16[4,512,256]{2,1,0:T(8,128)(2,1)}, u32[]{:S(2)}, u32[]{:S(2)}) collective-permute-start(bf16[4,512,256]{2,1,0:T(8,128)(2,1)} %slice.151), channel_id=1, source_target_pairs={{0,96},{1,33},{8,104},{9,41},{16,112},{17,49},{24,120},{25,57},{32... | collective-permute-start | bytes 3145736 | tf_op jit(solution)/shard_map/ppermute | solution.py:40
  149.0 7.3 %collective-permute-start.12 = (bf16[4,128,128]{2,1,0:T(8,128)(2,1)S(1)}, bf16[4,128,128]{2,1,0:T(8,128)(2,1)S(1)}, u32[]{:S(2)}, u32[]{:S(2)}) collective-permute-start(bf16[4,128,128]{2,1,0:T(8,128)(2,1)S(1)} %convert_element_type.136), channel_id=1, source_target_pairs={{0,8},{8,0},{16,24},{24,16},{1,9},{9,1},{17,25},{25,17},{2,10},{10... | collective-permute-start | bytes 393224 | tf_op jit(solution)/shard_map/ppermute | solution.py:29
  150.7 8.7 %collective-permute-start.13 = (bf16[4,128,128]{2,1,0:T(8,128)(2,1)S(1)}, bf16[4,128,128]{2,1,0:T(8,128)(2,1)S(1)}, u32[]{:S(2)}, u32[]{:S(2)}) collective-permute-start(bf16[4,128,128]{2,1,0:T(8,128)(2,1)S(1)} %convert_element_type.136), channel_id=1, source_target_pairs={{0,24},{8,16},{16,8},{24,0},{1,25},{9,17},{17,9},{25,1},{2,26},{10... | collective-permute-start | bytes 393224 | tf_op jit(solution)/shard_map/ppermute | solution.py:29
  150.7 8.7 %collective-permute-start.14 = (bf16[4,128,128]{2,1,0:T(8,128)(2,1)S(1)}, bf16[4,128,128]{2,1,0:T(8,128)(2,1)S(1)}, u32[]{:S(2)}, u32[]{:S(2)}) collective-permute-start(bf16[4,128,128]{2,1,0:T(8,128)(2,1)S(1)} %convert_element_type.136), channel_id=1, source_target_pairs={{0,16},{8,24},{16,0},{24,8},{1,17},{9,25},{17,1},{25,9},{2,18},{10... | collective-permute-start | bytes 393224 | tf_op jit(solution)/shard_map/ppermute | solution.py:29
  160.1 8.7 %collective-permute-start.17 = (bf16[4,128,128]{2,1,0:T(8,128)(2,1)}, bf16[4,128,128]{2,1,0:T(8,128)(2,1)}, u32[]{:S(2)}, u32[]{:S(2)}) collective-permute-start(bf16[4,128,128]{2,1,0:T(8,128)(2,1)} %fusion.3), channel_id=1, source_target_pairs={{0,64},{32,96},{64,0},{96,32},{1,65},{33,97},{65,1},{97,33},{2,66}... | collective-permute-start | bytes 393224 | tf_op jit(solution)/shard_map/ppermute | solution.py:29
  162.4 8.1 %collective-permute-start.16 = (bf16[4,128,128]{2,1,0:T(8,128)(2,1)}, bf16[4,128,128]{2,1,0:T(8,128)(2,1)}, u32[]{:S(2)}, u32[]{:S(2)}) collective-permute-start(bf16[4,128,128]{2,1,0:T(8,128)(2,1)} %fusion.3), channel_id=1, source_target_pairs={{0,96},{32,64},{64,32},{96,0},{1,97},{33,65},{65,33},{97,1},{2,98}... | collective-permute-start | bytes 393224 | tf_op jit(solution)/shard_map/ppermute | solution.py:29
  163.0 7.4 %collective-permute-start.15 = (bf16[4,128,128]{2,1,0:T(8,128)(2,1)}, bf16[4,128,128]{2,1,0:T(8,128)(2,1)}, u32[]{:S(2)}, u32[]{:S(2)}) collective-permute-start(bf16[4,128,128]{2,1,0:T(8,128)(2,1)} %fusion.3), channel_id=1, source_target_pairs={{0,32},{32,0},{64,96},{96,64},{1,33},{33,1},{65,97},{97,65},{2,34}... | collective-permute-start | bytes 393224 | tf_op jit(solution)/shard_map/ppermute | solution.py:29
  175.0 9.3 %collective-permute-start.18 = (bf16[4,128,128]{2,1,0:T(8,128)(2,1)S(1)}, bf16[4,128,128]{2,1,0:T(8,128)(2,1)S(1)}, u32[]{:S(2)}, u32[]{:S(2)}) collective-permute-start(bf16[4,128,128]{2,1,0:T(8,128)(2,1)S(1)} %convert_element_type.144), channel_id=1, source_target_pairs={{0,8},{8,0},{16,24},{24,16},{1,9},{9,1},{17,25},{25,17},{2,10},{10... | collective-permute-start | bytes 393224 | tf_op jit(solution)/shard_map/ppermute | solution.py:29
  175.1 9.2 %collective-permute-start.19 = (bf16[4,128,128]{2,1,0:T(8,128)(2,1)S(1)}, bf16[4,128,128]{2,1,0:T(8,128)(2,1)S(1)}, u32[]{:S(2)}, u32[]{:S(2)}) collective-permute-start(bf16[4,128,128]{2,1,0:T(8,128)(2,1)S(1)} %convert_element_type.144), channel_id=1, source_target_pairs={{0,24},{8,16},{16,8},{24,0},{1,25},{9,17},{17,9},{25,1},{2,26},{10... | collective-permute-start | bytes 393224 | tf_op jit(solution)/shard_map/ppermute | solution.py:29
  177.1 7.2 %collective-permute-start.20 = (bf16[4,128,128]{2,1,0:T(8,128)(2,1)S(1)}, bf16[4,128,128]{2,1,0:T(8,128)(2,1)S(1)}, u32[]{:S(2)}, u32[]{:S(2)}) collective-permute-start(bf16[4,128,128]{2,1,0:T(8,128)(2,1)S(1)} %convert_element_type.144), channel_id=1, source_target_pairs={{0,16},{8,24},{16,0},{24,8},{1,17},{9,25},{17,1},{25,9},{2,18},{10... | collective-permute-start | bytes 393224 | tf_op jit(solution)/shard_map/ppermute | solution.py:29
  187.0 7.2 %collective-permute-start.22 = (bf16[4,128,128]{2,1,0:T(8,128)(2,1)S(1)}, bf16[4,128,128]{2,1,0:T(8,128)(2,1)S(1)}, u32[]{:S(2)}, u32[]{:S(2)}) collective-permute-start(bf16[4,128,128]{2,1,0:T(8,128)(2,1)S(1)} %convert_add_fusion.4), channel_id=1, source_target_pairs={{0,96},{32,64},{64,32},{96,0},{1,97},{33,65},{65,33},{97,1},{2,98}... | collective-permute-start | bytes 393224 | tf_op jit(solution)/shard_map/ppermute | solution.py:29
  187.8 6.5 %collective-permute-start.21 = (bf16[4,128,128]{2,1,0:T(8,128)(2,1)S(1)}, bf16[4,128,128]{2,1,0:T(8,128)(2,1)S(1)}, u32[]{:S(2)}, u32[]{:S(2)}) collective-permute-start(bf16[4,128,128]{2,1,0:T(8,128)(2,1)S(1)} %convert_add_fusion.4), channel_id=1, source_target_pairs={{0,32},{32,0},{64,96},{96,64},{1,33},{33,1},{65,97},{97,65},{2,34}... | collective-permute-start | bytes 393224 | tf_op jit(solution)/shard_map/ppermute | solution.py:29
  203.7 9.4 %collective-permute-start.24 = (bf16[256,2048]{1,0:T(8,128)(2,1)}, bf16[256,2048]{1,0:T(8,128)(2,1)S(1)}, u32[]{:S(2)}, u32[]{:S(2)}) collective-permute-start(bf16[256,2048]{1,0:T(8,128)(2,1)} %get-tuple-element.59), channel_id=1, source_target_pairs={{0,1},{1,0},{2,3},{3,2},{4,5},{5,4},{6,7},{7,6},{8,9},{9,8},{10,11... | collective-permute-start | bytes 3145736 | tf_op jit(solution)/shard_map/ppermute | solution.py:29
  212.9 11.0 %collective-permute-start.28 = (bf16[256,2048]{1,0:T(8,128)(2,1)}, bf16[256,2048]{1,0:T(8,128)(2,1)S(1)}, u32[]{:S(2)}, u32[]{:S(2)}) collective-permute-start(bf16[256,2048]{1,0:T(8,128)(2,1)} %get-tuple-element.65), channel_id=1, source_target_pairs={{0,1},{1,0},{2,3},{3,2},{4,5},{5,4},{6,7},{7,6},{8,9},{9,8},{10,11... | collective-permute-start | bytes 3145736 | tf_op jit(solution)/shard_map/ppermute | solution.py:29
  213.3 12.4 %collective-permute-start.25 = (bf16[128,2048]{1,0:T(8,128)(2,1)S(1)}, bf16[128,2048]{1,0:T(8,128)(2,1)S(1)}, u32[]{:S(2)}, u32[]{:S(2)}) collective-permute-start(bf16[128,2048]{1,0:T(8,128)(2,1)S(1)} %add_convert_fusion.3), channel_id=1, source_target_pairs={{0,2},{1,7},{2,0},{3,5},{4,6},{5,3},{6,4},{7,1},{8,10},{9,15},{10,... | collective-permute-start | bytes 1572872 | tf_op jit(solution)/shard_map/ppermute | solution.py:330
  223.8 10.9 %collective-permute-start.27 = (bf16[256,2048]{1,0:T(8,128)(2,1)}, bf16[256,2048]{1,0:T(8,128)(2,1)S(1)}, u32[]{:S(2)}, u32[]{:S(2)}) collective-permute-start(bf16[256,2048]{1,0:T(8,128)(2,1)} %get-tuple-element.63), channel_id=1, source_target_pairs={{0,1},{1,0},{2,3},{3,2},{4,5},{5,4},{6,7},{7,6},{8,9},{9,8},{10,11... | collective-permute-start | bytes 3145736 | tf_op jit(solution)/shard_map/ppermute | solution.py:29
  224.1 12.1 %collective-permute-start.30 = (bf16[128,2048]{1,0:T(8,128)(2,1)S(1)}, bf16[128,2048]{1,0:T(8,128)(2,1)S(1)}, u32[]{:S(2)}, u32[]{:S(2)}) collective-permute-start(bf16[128,2048]{1,0:T(8,128)(2,1)S(1)} %add_convert_fusion.1), channel_id=1, source_target_pairs={{0,2},{1,7},{2,0},{3,5},{4,6},{5,3},{6,4},{7,1},{8,10},{9,15},{10,... | collective-permute-start | bytes 1572872 | tf_op jit(solution)/shard_map/ppermute | solution.py:330
  234.8 14.8 %collective-permute-start.32 = (bf16[128,2048]{1,0:T(8,128)(2,1)S(1)}, bf16[128,2048]{1,0:T(8,128)(2,1)S(1)}, u32[]{:S(2)}, u32[]{:S(2)}) collective-permute-start(bf16[128,2048]{1,0:T(8,128)(2,1)S(1)} %add_convert_fusion.2), channel_id=1, source_target_pairs={{0,2},{1,7},{2,0},{3,5},{4,6},{5,3},{6,4},{7,1},{8,10},{9,15},{10,... | collective-permute-start | bytes 1572872 | tf_op jit(solution)/shard_map/ppermute | solution.py:330
  236.4 13.5 %collective-permute-start.31 = (bf16[64,2048]{1,0:T(8,128)(2,1)S(1)}, bf16[64,2048]{1,0:T(8,128)(2,1)S(1)}, u32[]{:S(2)}, u32[]{:S(2)}) collective-permute-start(bf16[64,2048]{1,0:T(8,128)(2,1)S(1)} %slice.198), channel_id=1, source_target_pairs={{0,6},{1,3},{2,4},{3,1},{4,2},{5,7},{6,0},{7,5},{8,14},{9,11},{10,... | collective-permute-start | bytes 786440 | tf_op jit(solution)/shard_map/ppermute | solution.py:330
  236.7 19.6 %collective-permute-start.34 = (bf16[128,2048]{1,0:T(8,128)(2,1)S(1)}, bf16[128,2048]{1,0:T(8,128)(2,1)S(1)}, u32[]{:S(2)}, u32[]{:S(2)}) collective-permute-start(bf16[128,2048]{1,0:T(8,128)(2,1)S(1)} %add_convert_fusion), channel_id=1, source_target_pairs={{0,2},{1,7},{2,0},{3,5},{4,6},{5,3},{6,4},{7,1},{8,10},{9,15},{10,... | collective-permute-start | bytes 1572872 | tf_op jit(solution)/shard_map/ppermute | solution.py:330
  250.0 7.2 %collective-permute-start.33 = (bf16[64,2048]{1,0:T(8,128)(2,1)S(1)}, bf16[64,2048]{1,0:T(8,128)(2,1)S(1)}, u32[]{:S(2)}, u32[]{:S(2)}) collective-permute-start(bf16[64,2048]{1,0:T(8,128)(2,1)S(1)} %slice.197), channel_id=1, source_target_pairs={{0,6},{1,3},{2,4},{3,1},{4,2},{5,7},{6,0},{7,5},{8,14},{9,11},{10,... | collective-permute-start | bytes 786440 | tf_op jit(solution)/shard_map/ppermute | solution.py:330
  (23 other events, 195.6 us)

commit v3 on v2

--- a/solution.py
+++ b/solution.py
@@ -483,7 +483,7 @@
     wide = 2 * heads * DH
     sums = project(20, [held[0], near[0], held[1], near[1]], ((0, 0), (0, 4), (1, 0), (1, 4)), hid[0::3], (wide, wide // 2))
     sums = project(14, far, ((0, 0), (1, 0)), hid[1::3], (wide, wide // 2), sums)
-    pre_kv, own_state = project(44, last_kv, ((0, 0), (1, 0)), hid[2::3], (wide,), sums[:1], heads)
+    pre_kv, own_state = project(47, last_kv, ((0, 0), (1, 0)), hid[2::3], (wide,), sums[:1], heads)
     inner, total = state_round(own_state, "y", False)
     outer, _ = state_round(total, "z", False)
     before = inner + outer

time: 270 us -> 271 us (level)
  transfers between devices with their start and end apart: 36 -> 36, of which waited for: 18 -> 18; matrix products, arithmetic and copies ran while one was open for 6% -> 6% of each run, Pallas kernels for 20% -> 21%
where the time goes in v3:
time: 271 us; the launch traced here: 266 us
  waiting for transfers between devices  121 us (45%)
  Pallas kernels  69.2 us (26%)
  starting transfers between devices  38.7 us (14%)
  local copies, waits for them, and re-layouts  23.1 us (9%)
  other arithmetic  13 us (5%)
    ppermute x12, waiting for transfers between devices, swap_links(): return lax.ppermute(x, ('z', 'y', 'c'), pairs)  85.1 us
    pallas_call x3, Pallas kernels, push(): pl.pallas_call(functools.partial(push_kernel, kinds, counts), in_specs=[h...  23.3 us
    ppermute x8, waiting for transfers between devices, swap_rings(): return lax.ppermute(a, ('x', 'c'), pairs)  22.4 us
    pallas_call x4, Pallas kernels, project(): pl.pallas_call(functools.partial(project_kernel, slots, len(start), heads...  21.3 us
    ppermute x16, starting transfers between devices, swap(): return lax.ppermute(x, axis, [(i, i ^ offset) for i in range(n)])  15.9 us
    ppermute x12, starting transfers between devices, swap_links(): return lax.ppermute(x, ('z', 'y', 'c'), pairs)  14 us
    ppermute x16, waiting for transfers between devices, swap(): return lax.ppermute(x, axis, [(i, i ^ offset) for i in range(n)])  13.3 us
    unnamed x38, local copies, waits for them, and re-layouts  10.9 us
  transfers between devices with their start and end apart: 36, of which 18 were waited for; matrix products, arithmetic and copies ran while one was open for 6% of the time, Pallas kernels for 21%

profile of v3, /device:TPU:1, one launch (start us, length us, event | category | flops | bytes accessed | tf_op | source)
XLA Modules:
  0.0 265.8 jit_solution(4015755493976355965)
XLA Ops:
  3.0 3.6 %collective-permute-start.3 = (bf16[1,1536,256]{2,1,0:T(8,128)(2,1)S(1)}, bf16[1,1536,256]{2,1,0:T(8,128)(2,1)S(1)}, u32[]{:S(2)}, u32[]{:S(2)}) collective-permute-start(bf16[1,1536,256]{2,1,0:T(8,128)(2,1)S(1)} %get-tuple-element.76), channel_id=1, source_target_pairs={{0,8},{1,25},{8,0},{9,17},{16,24},{17,9},{24,16},{25,1},{32,40},{3... | collective-permute-start | bytes 2359304 | tf_op jit(solution)/shard_map/ppermute | solution.py:40
  6.6 3.8 %collective-permute-start = (bf16[1,1536,256]{2,1,0:T(8,128)(2,1)S(1)}, bf16[1,1536,256]{2,1,0:T(8,128)(2,1)S(1)}, u32[]{:S(2)}, u32[]{:S(2)}) collective-permute-start(bf16[1,1536,256]{2,1,0:T(8,128)(2,1)S(1)} %get-tuple-element.77), channel_id=1, source_target_pairs={{0,32},{1,97},{8,40},{9,105},{16,48},{17,113},{24,56},{25,121},{32... | collective-permute-start | bytes 2359304 | tf_op jit(solution)/shard_map/ppermute | solution.py:40
  10.4 5.6 %collective-permute-done.3 = bf16[1,1536,256]{2,1,0:T(8,128)(2,1)S(1)} collective-permute-done((bf16[1,1536,256]{2,1,0:T(8,128)(2,1)S(1)}, bf16[1,1536,256]{2,1,0:T(8,128)(2,1)S(1)}, u32[]{:S(2)}, u32[]{:S(2)}) %collective-permute-start.3) | collective-permute-done | bytes 786464 | tf_op jit(solution)/shard_map/ppermute | solution.py:40
  21.1 16.1 %collective-permute-done.4 = bf16[2,1536,256]{2,1,0:T(8,128)(2,1)} collective-permute-done((bf16[2,1536,256]{2,1,0:T(8,128)(2,1)}, bf16[2,1536,256]{2,1,0:T(8,128)(2,1)}, u32[]{:S(2)}, u32[]{:S(2)}) %collective-permute-start.4) | collective-permute-done | bytes 1572896 | tf_op jit(solution)/shard_map/ppermute | solution.py:40
  37.2 3.8 %collective-permute-done.1 = bf16[2,1536,256]{2,1,0:T(8,128)(2,1)} collective-permute-done((bf16[2,1536,256]{2,1,0:T(8,128)(2,1)}, bf16[2,1536,256]{2,1,0:T(8,128)(2,1)}, u32[]{:S(2)}, u32[]{:S(2)}) %collective-permute-start.1) | collective-permute-done | bytes 1572896 | tf_op jit(solution)/shard_map/ppermute | solution.py:40
  47.3 3.6 %collective-permute-start.5 = (bf16[4,1536,256]{2,1,0:T(8,128)(2,1)}, bf16[4,1536,256]{2,1,0:T(8,128)(2,1)}, u32[]{:S(2)}, u32[]{:S(2)}) collective-permute-start(bf16[4,1536,256]{2,1,0:T(8,128)(2,1)} %pad_maximum_fusion.1.refs_2_.refs_1_), channel_id=1, source_target_pairs={{0,32},{1,97},{8,40},{9,105},{16,48},{17,113},{24,56},{25,121},{32... | collective-permute-start | bytes 9437192 | tf_op jit(solution)/shard_map/ppermute | solution.py:40
  51.3 3.4 %copy-done.1 = bf16[512,8192]{1,0:T(8,128)(2,1)S(1)} copy-done((bf16[512,8192]{1,0:T(8,128)(2,1)S(1)}, bf16[512,8192]{1,0:T(8,128)(2,1)}, u32[]{:S(2)}) %copy-start.1) | copy-done | bytes 8388632
  54.7 6.5 %reorder_columns.1 = (bf16[8,256,512]{2,1,0:T(8,128)(2,1)S(1)}, bf16[4,256,512]{2,1,0:T(8,128)(2,1)S(1)}, bf16[4,256,512]{2,1,0:T(8,128)(2,1)S(1)}, bf16[8,256,5...) custom-call(s32[2,16]{1,0:T(2,128)S(1)} %pad_add_fusion.table, ...), custom_call_target="tpu_custom_call" | custom-call | bytes 16777216 | tf_op jit(solution)/shard_map/reorder_columns/pallas_call | solution.py:107
  62.2 37.5 %collective-permute-done.2.refs_1_ = bf16[4,1536,256]{2,1,0:T(8,128)(2,1)} collective-permute-done((bf16[4,1536,256]{2,1,0:T(8,128)(2,1)}, bf16[4,1536,256]{2,1,0:T(8,128)(2,1)}, u32[]{:S(2)}, u32[]{:S(2)}) %collective-permute-start.2) | collective-permute-done | bytes 3145760 | tf_op jit(solution)/shard_map/ppermute | solution.py:40
  101.5 3.3 %collective-permute-done.5.refs_3_.refs_1_ = bf16[4,1536,256]{2,1,0:T(8,128)(2,1)} collective-permute-done((bf16[4,1536,256]{2,1,0:T(8,128)(2,1)}, bf16[4,1536,256]{2,1,0:T(8,128)(2,1)}, u32[]{:S(2)}, u32[]{:S(2)}) %collective-permute-start.5) | collective-permute-done | bytes 3145760 | tf_op jit(solution)/shard_map/ppermute | solution.py:40
  106.7 2.3 slice.150
  112.3 7.5 %collective-permute-done.6.refs_2_ = bf16[4,1536,256]{2,1,0:T(8,128)(2,1)S(1)} collective-permute-done((bf16[4,1536,256]{2,1,0:T(8,128)(2,1)}, bf16[4,1536,256]{2,1,0:T(8,128)(2,1)S(1)}, u32[]{:S(2)}, u32[]{:S(2)}) %collective-permute-start.6) | collective-permute-done | bytes 3145760 | tf_op jit(solution)/shard_map/ppermute | solution.py:40
  120.0 10.1 %project.4 = (f32[1024,512]{1,0:T(8,128)S(1)}, f32[512,512]{1,0:T(8,128)S(1)}) custom-call(bf16[4,1536,256]{2,1,0:T(8,128)(2,1)} %pad_maximum_fusion.refs_0_, bf16[4,1536,256]{2,1,0:T(8,128)(2,1)} %collective-permute-done.2.refs_1_, bf16[4,1536,256]{2,1,0:T(8,128)(2,1)} %pad_maximum_fusion.1.refs_2_.refs_1_, ...), custom_call_target="tpu_custom_call" | custom-call | flops 6442450944 | bytes 12582912 | tf_op jit(solution)/shard_map/project/pallas_call | solution.py:218
  130.1 4.2 %project.5 = (f32[1024,512]{1,0:T(8,128)S(1)}, f32[512,512]{1,0:T(8,128)S(1)}) custom-call(f32[1024,512]{1,0:T(8,128)S(1)} %get-tuple-element.40.refs_0_, f32[512,512]{1,0:T(8,128)S(1)} %get-tuple-element.41.refs_1_, bf16[4,1536,256]{2,1,0:T(8,128)(2,1)S(1)} %collective-permute-done.6.refs_2_, ...), custom_call_target="tpu_custom_call" | custom-call | flops 3221225472 | bytes 6291456 | tf_op jit(solution)/shard_map/project/pallas_call | solution.py:218
  135.3 7.1 %collective-permute-done.8.refs_1_ = bf16[4,1024,256]{2,1,0:T(8,128)(2,1)S(1)} collective-permute-done((bf16[4,1024,256]{2,1,0:T(8,128)(2,1)S(1)}, bf16[4,1024,256]{2,1,0:T(8,128)(2,1)S(1)}, u32[]{:S(2)}, u32[]{:S(2)}) %collective-permute-start.8) | collective-permute-done | bytes 2097184 | tf_op jit(solution)/shard_map/ppermute | solution.py:40
  145.7 4.3 %project.6 = (f32[1024,512]{1,0:T(8,128)S(1)}, f32[4,128,128]{2,1,0:T(8,128)S(1)}) custom-call(f32[1024,512]{1,0:T(8,128)S(1)} %get-tuple-element.48.refs_0_, bf16[4,1024,256]{2,1,0:T(8,128)(2,1)} %copy-done.13, bf16[4,1024,256]{2,1,0:T(8,128)(2,1)} %copy-done.12, bf16[4,256,512]{2,1,0:T(8,128)(2,1)S(1)} %get-tuple-element.43.refs_3_, ...), custom_call_target="tpu_custom_call" | custom-call | flops 2147483648 | bytes 4194304 | tf_op jit(solution)/shard_map/project/pallas_call | solution.py:218
  153.7 2.6 collective-permute-done.12
  156.2 4.5 %collective-permute-done.13 = bf16[4,128,128]{2,1,0:T(8,128)(2,1)S(1)} collective-permute-done((bf16[4,128,128]{2,1,0:T(8,128)(2,1)S(1)}, bf16[4,128,128]{2,1,0:T(8,128)(2,1)S(1)}, u32[]{:S(2)}, u32[]{:S(2)}) %collective-permute-start.13) | collective-permute-done | bytes 131104 | tf_op jit(solution)/shard_map/ppermute | solution.py:29
  167.5 2.7 %project.7.pre_q = f32[512,512]{1,0:T(8,128)S(1)} custom-call(f32[512,512]{1,0:T(8,128)S(1)} %copy-done.5, bf16[4,512,256]{2,1,0:T(8,128)(2,1)} %collective-permute-done.10.refs_1_.refs_2_, bf16[4,512,256]{2,1,0:T(8,128)(2,1)} %collective-permute-done.11.refs_2_.refs_3_, bf16[4,256,512]{2,1,0:T(8,128)(2,1)S(1)} %get-tuple-element.43.refs_3_, ...), custom_call_target="tpu_custom_call" | custom-call | flops 1073741824 | bytes 2097152 | tf_op jit(solution)/shard_map/project/pallas_call | solution.py:218
  172.7 3.3 %attend.1 = (f32[4,128,128]{2,1,0:T(8,128)S(1)}, bf16[512,512]{1,0:T(8,128)(2,1)S(1)}) custom-call(f32[512,512]{1,0:T(8,128)S(1)} %project.7.pre_q, f32[1024,512]{1,0:T(8,128)S(1)} %get-tuple-element.49.pre_k.pre_v.pre_kv, f32[1024,512]{1,0:T(8,128)S(1)} %get-tuple-element.49.pre_k.pre_v.pre_kv, f32[4,128,128]{2,1,0:T(8,128)S(1)} %fusion.2.before, ...), custom_call_target="tpu_custom_call" | custom-call | tf_op jit(solution)/shard_map/attend/pallas_call | solution.py:281
  176.9 2.7 %collective-permute-start.20 = (bf16[4,128,128]{2,1,0:T(8,128)(2,1)S(1)}, bf16[4,128,128]{2,1,0:T(8,128)(2,1)S(1)}, u32[]{:S(2)}, u32[]{:S(2)}) collective-permute-start(bf16[4,128,128]{2,1,0:T(8,128)(2,1)S(1)} %convert_element_type.144), channel_id=1, source_target_pairs={{0,16},{8,24},{16,0},{24,8},{1,17},{9,25},{17,1},{25,9},{2,18},{10... | collective-permute-start | bytes 393224 | tf_op jit(solution)/shard_map/ppermute | solution.py:29
  179.6 3.8 %attend_back.1 = (bf16[512,512]{1,0:T(8,128)(2,1)S(1)}, f32[512,512]{1,0:T(8,128)S(1)}, f32[512,512]{1,0:T(8,128)S(1)}) custom-call(f32[512,512]{1,0:T(8,128)S(1)} %project.7.pre_q, f32[1024,512]{1,0:T(8,128)S(1)} %get-tuple-element.49.pre_k.pre_v.pre_kv, f32[1024,512]{1,0:T(8,128)S(1)} %get-tuple-element.49.pre_k.pre_v.pre_kv, ...), custom_call_target="tpu_custom_call" | custom-call | flops 805306368 | bytes 4194304 | tf_op jit(solution)/shard_map/attend_back/pallas_call | solution.py:299
  191.5 3.1 %collective-permute-done.22 = bf16[4,128,128]{2,1,0:T(8,128)(2,1)S(1)} collective-permute-done((bf16[4,128,128]{2,1,0:T(8,128)(2,1)S(1)}, bf16[4,128,128]{2,1,0:T(8,128)(2,1)S(1)}, u32[]{:S(2)}, u32[]{:S(2)}) %collective-permute-start.22) | collective-permute-done | bytes 131104 | tf_op jit(solution)/shard_map/ppermute | solution.py:29
  195.4 8.6 %collect.1 = (bf16[512,1536]{1,0:T(8,128)(2,1)}, bf16[256,2048]{1,0:T(8,128)(2,1)}, bf16[256,2048]{1,0:T(8,128)(2,1)}) custom-call(s32[8]{0:T(128)} %stack.308.table, f32[1024,512]{1,0:T(8,128)} %copy-done, f32[512,512]{1,0:T(8,128)} %copy-done.9, f32[512,512]{1,0:T(8,128)} %copy-done.10, bf16[512,512]{1,0:T(8,128)(2,1)} %copy-done.11, ...), custom_call_target="tpu_custom_call" | custom-call | flops 3221225472 | bytes 6291456 | tf_op jit(solution)/shard_map/collect/pallas_call | solution.py:408
  206.2 7.7 %push.4 = (bf16[256,2048]{1,0:T(8,128)(2,1)}, bf16[256,2048]{1,0:T(8,128)(2,1)}) custom-call(bf16[512,1536]{1,0:T(8,128)(2,1)} %get-tuple-element.66.refs_0_, bf16[4,1536,256]{2,1,0:T(8,128)(2,1)} %collective-permute-done.2.refs_1_, bf16[4,1536,256]{2,1,0:T(8,128)(2,1)} %copy-done.8), custom_call_target="tpu_custom_call" | custom-call | flops 3221225472 | bytes 1 | tf_op jit(solution)/shard_map/push/pallas_call | solution.py:459
  214.3 2.6 collective-permute-start.25
  216.9 7.9 %push.3 = (bf16[256,2048]{1,0:T(8,128)(2,1)}, bf16[256,2048]{1,0:T(8,128)(2,1)}) custom-call(bf16[512,1536]{1,0:T(8,128)(2,1)} %get-tuple-element.66.refs_0_, bf16[4,1536,256]{2,1,0:T(8,128)(2,1)} %pad_maximum_fusion.1.refs_2_.refs_1_, bf16[4,1024,256]{2,1,0:T(8,128)(2,1)} %copy-done.12, bf16[4,512,256]{2,1,0:T(8,128)(2,1)} %collective-permute-done.11.refs_2_.refs_3_), custom_call_target="tpu_custom_call" | custom-call | flops 3221225472 | bytes 1 | tf_op jit(solution)/shard_map/push/pallas_call | solution.py:459
  226.7 7.7 %push.5 = (bf16[256,2048]{1,0:T(8,128)(2,1)}, bf16[256,2048]{1,0:T(8,128)(2,1)}) custom-call(bf16[512,1536]{1,0:T(8,128)(2,1)} %get-tuple-element.66.refs_0_, bf16[4,1536,256]{2,1,0:T(8,128)(2,1)} %collective-permute-done.5.refs_3_.refs_1_, bf16[4,1536,256]{2,1,0:T(8,128)(2,1)} %copy-done.7), custom_call_target="tpu_custom_call" | custom-call | flops 3221225472 | bytes 1 | tf_op jit(solution)/shard_map/push/pallas_call | solution.py:459
  240.3 10.4 %collective-permute-done.32 = bf16[128,2048]{1,0:T(8,128)(2,1)S(1)} collective-permute-done((bf16[128,2048]{1,0:T(8,128)(2,1)S(1)}, bf16[128,2048]{1,0:T(8,128)(2,1)S(1)}, u32[]{:S(2)}, u32[]{:S(2)}) %collective-permute-start.32) | collective-permute-done | bytes 524320 | tf_op jit(solution)/shard_map/ppermute | solution.py:330
  251.2 6.2 %collective-permute-done.34 = bf16[128,2048]{1,0:T(8,128)(2,1)S(1)} collective-permute-done((bf16[128,2048]{1,0:T(8,128)(2,1)S(1)}, bf16[128,2048]{1,0:T(8,128)(2,1)S(1)}, u32[]{:S(2)}, u32[]{:S(2)}) %collective-permute-start.34) | collective-permute-done | bytes 524320 | tf_op jit(solution)/shard_map/ppermute | solution.py:330
  258.2 4.7 %collective-permute-done.35 = bf16[64,2048]{1,0:T(8,128)(2,1)S(1)} collective-permute-done((bf16[64,2048]{1,0:T(8,128)(2,1)S(1)}, bf16[64,2048]{1,0:T(8,128)(2,1)S(1)}, u32[]{:S(2)}, u32[]{:S(2)}) %collective-permute-start.35) | collective-permute-done | bytes 262176 | tf_op jit(solution)/shard_map/ppermute | solution.py:330
  263.0 2.3 finish.1
  (134 shorter events, 61.3 us)
Async XLA Ops:
  3.0 13.0 %collective-permute-start.3 = (bf16[1,1536,256]{2,1,0:T(8,128)(2,1)S(1)}, bf16[1,1536,256]{2,1,0:T(8,128)(2,1)S(1)}, u32[]{:S(2)}, u32[]{:S(2)}) collective-permute-start(bf16[1,1536,256]{2,1,0:T(8,128)(2,1)S(1)} %get-tuple-element.76), channel_id=1, source_target_pairs={{0,8},{1,25},{8,0},{9,17},{16,24},{17,9},{24,16},{25,1},{32,40},{3... | collective-permute-start | bytes 2359304 | tf_op jit(solution)/shard_map/ppermute | solution.py:40
  6.6 13.1 %collective-permute-start = (bf16[1,1536,256]{2,1,0:T(8,128)(2,1)S(1)}, bf16[1,1536,256]{2,1,0:T(8,128)(2,1)S(1)}, u32[]{:S(2)}, u32[]{:S(2)}) collective-permute-start(bf16[1,1536,256]{2,1,0:T(8,128)(2,1)S(1)} %get-tuple-element.77), channel_id=1, source_target_pairs={{0,32},{1,97},{8,40},{9,105},{16,48},{17,113},{24,56},{25,121},{32... | collective-permute-start | bytes 2359304 | tf_op jit(solution)/shard_map/ppermute | solution.py:40
  17.3 19.9 %collective-permute-start.4 = (bf16[2,1536,256]{2,1,0:T(8,128)(2,1)}, bf16[2,1536,256]{2,1,0:T(8,128)(2,1)}, u32[]{:S(2)}, u32[]{:S(2)}) collective-permute-start(bf16[2,1536,256]{2,1,0:T(8,128)(2,1)} %pad_maximum_fusion.4), channel_id=1, source_target_pairs={{0,24},{1,9},{8,16},{9,1},{16,8},{17,25},{24,0},{25,17},{32,56},{3... | collective-permute-start | bytes 4718600 | tf_op jit(solution)/shard_map/ppermute | solution.py:40
  21.1 19.9 %collective-permute-start.1 = (bf16[2,1536,256]{2,1,0:T(8,128)(2,1)}, bf16[2,1536,256]{2,1,0:T(8,128)(2,1)}, u32[]{:S(2)}, u32[]{:S(2)}) collective-permute-start(bf16[2,1536,256]{2,1,0:T(8,128)(2,1)} %pad_maximum_fusion.3), channel_id=1, source_target_pairs={{0,96},{1,33},{8,104},{9,41},{16,112},{17,49},{24,120},{25,57},{32... | collective-permute-start | bytes 4718600 | tf_op jit(solution)/shard_map/ppermute | solution.py:40
  45.1 54.6 %collective-permute-start.2 = (bf16[4,1536,256]{2,1,0:T(8,128)(2,1)}, bf16[4,1536,256]{2,1,0:T(8,128)(2,1)}, u32[]{:S(2)}, u32[]{:S(2)}) collective-permute-start(bf16[4,1536,256]{2,1,0:T(8,128)(2,1)} %pad_maximum_fusion.refs_0_), channel_id=1, source_target_pairs={{0,8},{1,25},{8,0},{9,17},{16,24},{17,9},{24,16},{25,1},{32,40},{3... | collective-permute-start | bytes 9437192 | tf_op jit(solution)/shard_map/ppermute | solution.py:40
  47.3 57.6 %collective-permute-start.5 = (bf16[4,1536,256]{2,1,0:T(8,128)(2,1)}, bf16[4,1536,256]{2,1,0:T(8,128)(2,1)}, u32[]{:S(2)}, u32[]{:S(2)}) collective-permute-start(bf16[4,1536,256]{2,1,0:T(8,128)(2,1)} %pad_maximum_fusion.1.refs_2_.refs_1_), channel_id=1, source_target_pairs={{0,32},{1,97},{8,40},{9,105},{16,48},{17,113},{24,56},{25,121},{32... | collective-permute-start | bytes 9437192 | tf_op jit(solution)/shard_map/ppermute | solution.py:40
  61.2 58.6 %collective-permute-start.6 = (bf16[4,1536,256]{2,1,0:T(8,128)(2,1)}, bf16[4,1536,256]{2,1,0:T(8,128)(2,1)S(1)}, u32[]{:S(2)}, u32[]{:S(2)}) collective-permute-start(bf16[4,1536,256]{2,1,0:T(8,128)(2,1)} %pad_maximum_fusion.refs_0_), channel_id=1, source_target_pairs={{0,24},{1,9},{8,16},{9,1},{16,8},{17,25},{24,0},{25,17},{32,56},{3... | collective-permute-start | bytes 9437192 | tf_op jit(solution)/shard_map/ppermute | solution.py:40
  62.2 67.9 %collective-permute-start.7 = (bf16[4,1536,256]{2,1,0:T(8,128)(2,1)}, bf16[4,1536,256]{2,1,0:T(8,128)(2,1)S(1)}, u32[]{:S(2)}, u32[]{:S(2)}) collective-permute-start(bf16[4,1536,256]{2,1,0:T(8,128)(2,1)} %pad_maximum_fusion.1.refs_2_.refs_1_), channel_id=1, source_target_pairs={{0,96},{1,33},{8,104},{9,41},{16,112},{17,49},{24,120},{25,57},{32... | collective-permute-start | bytes 9437192 | tf_op jit(solution)/shard_map/ppermute | solution.py:40
  101.4 41.0 %collective-permute-start.8 = (bf16[4,1024,256]{2,1,0:T(8,128)(2,1)S(1)}, bf16[4,1024,256]{2,1,0:T(8,128)(2,1)S(1)}, u32[]{:S(2)}, u32[]{:S(2)}) collective-permute-start(bf16[4,1024,256]{2,1,0:T(8,128)(2,1)S(1)} %slice.148), channel_id=1, source_target_pairs={{0,24},{1,9},{8,16},{9,1},{16,8},{17,25},{24,0},{25,17},{32,56},{3... | collective-permute-start | bytes 6291464 | tf_op jit(solution)/shard_map/ppermute | solution.py:40
  106.6 37.8 %collective-permute-start.9 = (bf16[4,1024,256]{2,1,0:T(8,128)(2,1)S(1)}, bf16[4,1024,256]{2,1,0:T(8,128)(2,1)S(1)}, u32[]{:S(2)}, u32[]{:S(2)}) collective-permute-start(bf16[4,1024,256]{2,1,0:T(8,128)(2,1)S(1)} %slice.149), channel_id=1, source_target_pairs={{0,96},{1,33},{8,104},{9,41},{16,112},{17,49},{24,120},{25,57},{32... | collective-permute-start | bytes 6291464 | tf_op jit(solution)/shard_map/ppermute | solution.py:40
  109.0 56.0 %collective-permute-start.10 = (bf16[4,512,256]{2,1,0:T(8,128)(2,1)}, bf16[4,512,256]{2,1,0:T(8,128)(2,1)}, u32[]{:S(2)}, u32[]{:S(2)}) collective-permute-start(bf16[4,512,256]{2,1,0:T(8,128)(2,1)} %slice.150), channel_id=1, source_target_pairs={{0,24},{1,9},{8,16},{9,1},{16,8},{17,25},{24,0},{25,17},{32,56},{3... | collective-permute-start | bytes 3145736 | tf_op jit(solution)/shard_map/ppermute | solution.py:40
  119.8 45.2 %collective-permute-start.11 = (bf16[4,512,256]{2,1,0:T(8,128)(2,1)}, bf16[4,512,256]{2,1,0:T(8,128)(2,1)}, u32[]{:S(2)}, u32[]{:S(2)}) collective-permute-start(bf16[4,512,256]{2,1,0:T(8,128)(2,1)} %slice.151), channel_id=1, source_target_pairs={{0,96},{1,33},{8,104},{9,41},{16,112},{17,49},{24,120},{25,57},{32... | collective-permute-start | bytes 3145736 | tf_op jit(solution)/shard_map/ppermute | solution.py:40
  150.1 6.1 %collective-permute-start.12 = (bf16[4,128,128]{2,1,0:T(8,128)(2,1)S(1)}, bf16[4,128,128]{2,1,0:T(8,128)(2,1)S(1)}, u32[]{:S(2)}, u32[]{:S(2)}) collective-permute-start(bf16[4,128,128]{2,1,0:T(8,128)(2,1)S(1)} %convert_element_type.136), channel_id=1, source_target_pairs={{0,8},{8,0},{16,24},{24,16},{1,9},{9,1},{17,25},{25,17},{2,10},{10... | collective-permute-start | bytes 393224 | tf_op jit(solution)/shard_map/ppermute | solution.py:29
  151.8 9.0 %collective-permute-start.13 = (bf16[4,128,128]{2,1,0:T(8,128)(2,1)S(1)}, bf16[4,128,128]{2,1,0:T(8,128)(2,1)S(1)}, u32[]{:S(2)}, u32[]{:S(2)}) collective-permute-start(bf16[4,128,128]{2,1,0:T(8,128)(2,1)S(1)} %convert_element_type.136), channel_id=1, source_target_pairs={{0,24},{8,16},{16,8},{24,0},{1,25},{9,17},{17,9},{25,1},{2,26},{10... | collective-permute-start | bytes 393224 | tf_op jit(solution)/shard_map/ppermute | solution.py:29
  151.8 9.0 %collective-permute-start.14 = (bf16[4,128,128]{2,1,0:T(8,128)(2,1)S(1)}, bf16[4,128,128]{2,1,0:T(8,128)(2,1)S(1)}, u32[]{:S(2)}, u32[]{:S(2)}) collective-permute-start(bf16[4,128,128]{2,1,0:T(8,128)(2,1)S(1)} %convert_element_type.136), channel_id=1, source_target_pairs={{0,16},{8,24},{16,0},{24,8},{1,17},{9,25},{17,1},{25,9},{2,18},{10... | collective-permute-start | bytes 393224 | tf_op jit(solution)/shard_map/ppermute | solution.py:29
  161.5 8.7 %collective-permute-start.17 = (bf16[4,128,128]{2,1,0:T(8,128)(2,1)}, bf16[4,128,128]{2,1,0:T(8,128)(2,1)}, u32[]{:S(2)}, u32[]{:S(2)}) collective-permute-start(bf16[4,128,128]{2,1,0:T(8,128)(2,1)} %fusion.3), channel_id=1, source_target_pairs={{0,64},{32,96},{64,0},{96,32},{1,65},{33,97},{65,1},{97,33},{2,66}... | collective-permute-start | bytes 393224 | tf_op jit(solution)/shard_map/ppermute | solution.py:29
  163.4 8.1 %collective-permute-start.16 = (bf16[4,128,128]{2,1,0:T(8,128)(2,1)}, bf16[4,128,128]{2,1,0:T(8,128)(2,1)}, u32[]{:S(2)}, u32[]{:S(2)}) collective-permute-start(bf16[4,128,128]{2,1,0:T(8,128)(2,1)} %fusion.3), channel_id=1, source_target_pairs={{0,96},{32,64},{64,32},{96,0},{1,97},{33,65},{65,33},{97,1},{2,98}... | collective-permute-start | bytes 393224 | tf_op jit(solution)/shard_map/ppermute | solution.py:29
  164.4 7.1 %collective-permute-start.15 = (bf16[4,128,128]{2,1,0:T(8,128)(2,1)}, bf16[4,128,128]{2,1,0:T(8,128)(2,1)}, u32[]{:S(2)}, u32[]{:S(2)}) collective-permute-start(bf16[4,128,128]{2,1,0:T(8,128)(2,1)} %fusion.3), channel_id=1, source_target_pairs={{0,32},{32,0},{64,96},{96,64},{1,33},{33,1},{65,97},{97,65},{2,34}... | collective-permute-start | bytes 393224 | tf_op jit(solution)/shard_map/ppermute | solution.py:29
  176.1 9.3 %collective-permute-start.18 = (bf16[4,128,128]{2,1,0:T(8,128)(2,1)S(1)}, bf16[4,128,128]{2,1,0:T(8,128)(2,1)S(1)}, u32[]{:S(2)}, u32[]{:S(2)}) collective-permute-start(bf16[4,128,128]{2,1,0:T(8,128)(2,1)S(1)} %convert_element_type.144), channel_id=1, source_target_pairs={{0,8},{8,0},{16,24},{24,16},{1,9},{9,1},{17,25},{25,17},{2,10},{10... | collective-permute-start | bytes 393224 | tf_op jit(solution)/shard_map/ppermute | solution.py:29
  176.2 9.2 %collective-permute-start.19 = (bf16[4,128,128]{2,1,0:T(8,128)(2,1)S(1)}, bf16[4,128,128]{2,1,0:T(8,128)(2,1)S(1)}, u32[]{:S(2)}, u32[]{:S(2)}) collective-permute-start(bf16[4,128,128]{2,1,0:T(8,128)(2,1)S(1)} %convert_element_type.144), channel_id=1, source_target_pairs={{0,24},{8,16},{16,8},{24,0},{1,25},{9,17},{17,9},{25,1},{2,26},{10... | collective-permute-start | bytes 393224 | tf_op jit(solution)/shard_map/ppermute | solution.py:29
  176.9 8.5 %collective-permute-start.20 = (bf16[4,128,128]{2,1,0:T(8,128)(2,1)S(1)}, bf16[4,128,128]{2,1,0:T(8,128)(2,1)S(1)}, u32[]{:S(2)}, u32[]{:S(2)}) collective-permute-start(bf16[4,128,128]{2,1,0:T(8,128)(2,1)S(1)} %convert_element_type.144), channel_id=1, source_target_pairs={{0,16},{8,24},{16,0},{24,8},{1,17},{9,25},{17,1},{25,9},{2,18},{10... | collective-permute-start | bytes 393224 | tf_op jit(solution)/shard_map/ppermute | solution.py:29
  188.1 6.5 %collective-permute-start.22 = (bf16[4,128,128]{2,1,0:T(8,128)(2,1)S(1)}, bf16[4,128,128]{2,1,0:T(8,128)(2,1)S(1)}, u32[]{:S(2)}, u32[]{:S(2)}) collective-permute-start(bf16[4,128,128]{2,1,0:T(8,128)(2,1)S(1)} %convert_add_fusion.4), channel_id=1, source_target_pairs={{0,96},{32,64},{64,32},{96,0},{1,97},{33,65},{65,33},{97,1},{2,98}... | collective-permute-start | bytes 393224 | tf_op jit(solution)/shard_map/ppermute | solution.py:29
  188.8 5.8 %collective-permute-start.21 = (bf16[4,128,128]{2,1,0:T(8,128)(2,1)S(1)}, bf16[4,128,128]{2,1,0:T(8,128)(2,1)S(1)}, u32[]{:S(2)}, u32[]{:S(2)}) collective-permute-start(bf16[4,128,128]{2,1,0:T(8,128)(2,1)S(1)} %convert_add_fusion.4), channel_id=1, source_target_pairs={{0,32},{32,0},{64,96},{96,64},{1,33},{33,1},{65,97},{97,65},{2,34}... | collective-permute-start | bytes 393224 | tf_op jit(solution)/shard_map/ppermute | solution.py:29
  204.1 10.1 %collective-permute-start.24 = (bf16[256,2048]{1,0:T(8,128)(2,1)}, bf16[256,2048]{1,0:T(8,128)(2,1)S(1)}, u32[]{:S(2)}, u32[]{:S(2)}) collective-permute-start(bf16[256,2048]{1,0:T(8,128)(2,1)} %get-tuple-element.59), channel_id=1, source_target_pairs={{0,1},{1,0},{2,3},{3,2},{4,5},{5,4},{6,7},{7,6},{8,9},{9,8},{10,11... | collective-permute-start | bytes 3145736 | tf_op jit(solution)/shard_map/ppermute | solution.py:29
  213.9 11.0 %collective-permute-start.28 = (bf16[256,2048]{1,0:T(8,128)(2,1)}, bf16[256,2048]{1,0:T(8,128)(2,1)S(1)}, u32[]{:S(2)}, u32[]{:S(2)}) collective-permute-start(bf16[256,2048]{1,0:T(8,128)(2,1)} %get-tuple-element.65), channel_id=1, source_target_pairs={{0,1},{1,0},{2,3},{3,2},{4,5},{5,4},{6,7},{7,6},{8,9},{9,8},{10,11... | collective-permute-start | bytes 3145736 | tf_op jit(solution)/shard_map/ppermute | solution.py:29
  214.3 12.4 %collective-permute-start.25 = (bf16[128,2048]{1,0:T(8,128)(2,1)S(1)}, bf16[128,2048]{1,0:T(8,128)(2,1)S(1)}, u32[]{:S(2)}, u32[]{:S(2)}) collective-permute-start(bf16[128,2048]{1,0:T(8,128)(2,1)S(1)} %add_convert_fusion.3), channel_id=1, source_target_pairs={{0,2},{1,7},{2,0},{3,5},{4,6},{5,3},{6,4},{7,1},{8,10},{9,15},{10,... | collective-permute-start | bytes 1572872 | tf_op jit(solution)/shard_map/ppermute | solution.py:330
  224.8 10.9 %collective-permute-start.27 = (bf16[256,2048]{1,0:T(8,128)(2,1)}, bf16[256,2048]{1,0:T(8,128)(2,1)S(1)}, u32[]{:S(2)}, u32[]{:S(2)}) collective-permute-start(bf16[256,2048]{1,0:T(8,128)(2,1)} %get-tuple-element.63), channel_id=1, source_target_pairs={{0,1},{1,0},{2,3},{3,2},{4,5},{5,4},{6,7},{7,6},{8,9},{9,8},{10,11... | collective-permute-start | bytes 3145736 | tf_op jit(solution)/shard_map/ppermute | solution.py:29
  225.1 12.1 %collective-permute-start.30 = (bf16[128,2048]{1,0:T(8,128)(2,1)S(1)}, bf16[128,2048]{1,0:T(8,128)(2,1)S(1)}, u32[]{:S(2)}, u32[]{:S(2)}) collective-permute-start(bf16[128,2048]{1,0:T(8,128)(2,1)S(1)} %add_convert_fusion.1), channel_id=1, source_target_pairs={{0,2},{1,7},{2,0},{3,5},{4,6},{5,3},{6,4},{7,1},{8,10},{9,15},{10,... | collective-permute-start | bytes 1572872 | tf_op jit(solution)/shard_map/ppermute | solution.py:330
  235.9 14.9 %collective-permute-start.32 = (bf16[128,2048]{1,0:T(8,128)(2,1)S(1)}, bf16[128,2048]{1,0:T(8,128)(2,1)S(1)}, u32[]{:S(2)}, u32[]{:S(2)}) collective-permute-start(bf16[128,2048]{1,0:T(8,128)(2,1)S(1)} %add_convert_fusion.2), channel_id=1, source_target_pairs={{0,2},{1,7},{2,0},{3,5},{4,6},{5,3},{6,4},{7,1},{8,10},{9,15},{10,... | collective-permute-start | bytes 1572872 | tf_op jit(solution)/shard_map/ppermute | solution.py:330
  237.4 13.6 %collective-permute-start.31 = (bf16[64,2048]{1,0:T(8,128)(2,1)S(1)}, bf16[64,2048]{1,0:T(8,128)(2,1)S(1)}, u32[]{:S(2)}, u32[]{:S(2)}) collective-permute-start(bf16[64,2048]{1,0:T(8,128)(2,1)S(1)} %slice.198), channel_id=1, source_target_pairs={{0,6},{1,3},{2,4},{3,1},{4,2},{5,7},{6,0},{7,5},{8,14},{9,11},{10,... | collective-permute-start | bytes 786440 | tf_op jit(solution)/shard_map/ppermute | solution.py:330
  237.7 19.6 %collective-permute-start.34 = (bf16[128,2048]{1,0:T(8,128)(2,1)S(1)}, bf16[128,2048]{1,0:T(8,128)(2,1)S(1)}, u32[]{:S(2)}, u32[]{:S(2)}) collective-permute-start(bf16[128,2048]{1,0:T(8,128)(2,1)S(1)} %add_convert_fusion), channel_id=1, source_target_pairs={{0,2},{1,7},{2,0},{3,5},{4,6},{5,3},{6,4},{7,1},{8,10},{9,15},{10,... | collective-permute-start | bytes 1572872 | tf_op jit(solution)/shard_map/ppermute | solution.py:330
  251.1 7.1 %collective-permute-start.33 = (bf16[64,2048]{1,0:T(8,128)(2,1)S(1)}, bf16[64,2048]{1,0:T(8,128)(2,1)S(1)}, u32[]{:S(2)}, u32[]{:S(2)}) collective-permute-start(bf16[64,2048]{1,0:T(8,128)(2,1)S(1)} %slice.197), channel_id=1, source_target_pairs={{0,6},{1,3},{2,4},{3,1},{4,2},{5,7},{6,0},{7,5},{8,14},{9,11},{10,... | collective-permute-start | bytes 786440 | tf_op jit(solution)/shard_map/ppermute | solution.py:330
  (23 other events, 189.3 us)
